TPU v7x, 512 devices: a whole 4x4x16 slice. The times are simulated.
512 devices in a mesh: dp: 16 (over y, x), context: 32 (over z, core).
Axes of the slice: x: 4, y: 4, z: 16, core: 2. Of those that a mesh axis runs over, the one named last changes fastest.
Arguments:
- queries: bfloat16 [131072, 2048], P(('dp', 'context')), may hold values from -6 to 6
- keys: bfloat16 [32768, 512], P(('dp', 'context')), may hold values from -6 to 6
- values: bfloat16 [32768, 512], P(('dp', 'context')), may hold values from -6 to 6
- grad_out: bfloat16 [131072, 2048], P(('dp', 'context')), may hold values from -6 to 6
- layout: int32 [16, 128, 4], replicated, may hold values from 0 to 31, as said below
- counts: int32 [16], replicated, may hold values from 1 to 4, as said below
Outputs:
- attended: bfloat16 [131072, 2048], P(('dp', 'context'))
- query_gradient: bfloat16 [131072, 2048], P(('dp', 'context'))
- key_gradient: bfloat16 [32768, 512], P(('dp', 'context'))
- value_gradient: bfloat16 [32768, 512], P(('dp', 'context'))
Inputs may be any that keep to these rules, and one draw needn't show every extreme that they name: layout[h, b] lists 4 different key blocks of the sequence for query block b of head h, of which the first counts[h] are attended. Every query block of head h attends counts[h] key blocks; some head attends 4.
All inputs are finite; a program needn't handle non-finite values.
Results may differ from a plain program's by a relative error of at most 0.019.
Values may be sent and summed in bfloat16 or wider, within the bound.
A program may use at most 64 MiB of HBM per device.

v0:
```python
import math

import jax
import jax.numpy as jnp
from jax import lax
from jax.sharding import PartitionSpec as P

QUERY_HEADS = 16
KEY_VALUE_HEADS = 4
HEAD_WIDTH = 128
LAYOUT_BLOCK = 128
MAX_PICKED = 4


def swapped(block, axis, distance):
    count = lax.axis_size(axis)
    route = []
    for low in range(count):
        high = low | 1 << distance
        if high != low and high < count:
            route += [(low, high), (high, low)]
    return lax.ppermute(block, axis, route)


def owner_rows(token_rows, context_size, holder_split, query_portions):
    part_rows = token_rows.shape[0] // query_portions
    arranged = token_rows.reshape(query_portions, part_rows, QUERY_HEADS, HEAD_WIDTH).transpose(
        2, 0, 1, 3
    )
    return arranged.reshape(context_size, holder_split * part_rows, HEAD_WIDTH)


def token_rows_back(received, query_portions):
    part_rows = received.shape[0] * received.shape[1] // (QUERY_HEADS * query_portions)
    arranged = received.reshape(QUERY_HEADS, query_portions, part_rows, HEAD_WIDTH).transpose(
        1, 2, 0, 3
    )
    return arranged.reshape(query_portions * part_rows, QUERY_HEADS * HEAD_WIDTH)


def in_order(own_part, partner, member, axis_index):
    return jnp.where(
        member == 0,
        jnp.concatenate([own_part, partner], axis_index),
        jnp.concatenate([partner, own_part], axis_index),
    )


def head_pieces(stacked_rows, group_holders, context_size):
    stacking_depth = stacked_rows.shape[0]
    key_number = stacked_rows.shape[1]
    head_sorted = stacked_rows.reshape(stacking_depth, key_number, KEY_VALUE_HEADS, HEAD_WIDTH)
    arranged = jnp.repeat(head_sorted.transpose(2, 0, 1, 3), group_holders, axis=0)
    result_rows = arranged.reshape(context_size, stacking_depth * key_number, HEAD_WIDTH)
    return result_rows


def attend_item(
    query_item, grad_item, picked, head_count, key_tiles, value_tiles, key_accum, value_accum
):
    softmax_scale = 1.0 / math.sqrt(HEAD_WIDTH)
    tile_rows = query_item.shape[1]
    group_count = query_item.shape[0] // 4

    def one_group(group_step, loop_state):
        attended, query_gradient, key_total, value_total = loop_state
        query_tile = lax.dynamic_slice_in_dim(query_item, group_step * 4, 4, 0)
        grad_tile = lax.dynamic_slice_in_dim(grad_item, group_step * 4, 4, 0)
        chosen = lax.dynamic_slice_in_dim(picked, group_step * 4, 4, 0)

        def statistics(column, carried):
            running_max, running_sum, score_store = carried
            blocks = lax.dynamic_index_in_dim(chosen, column, 1, keepdims=False)
            key_tile = jnp.take(key_tiles, blocks, axis=0)
            score_matrix = (
                jnp.einsum("gqd,gkd->gqk", query_tile, key_tile, preferred_element_type=jnp.float32)
                * softmax_scale
            )
            new_max = jnp.maximum(running_max, jnp.max(score_matrix, axis=-1))
            running_sum = running_sum * jnp.exp(running_max - new_max) + jnp.sum(
                jnp.exp(score_matrix - new_max[..., None]), axis=-1
            )
            score_store = lax.dynamic_update_index_in_dim(score_store, score_matrix, column, 2)
            return (new_max, running_sum, score_store)

        initial = (
            jnp.full((4, tile_rows), -1e30, jnp.float32),
            jnp.zeros((4, tile_rows), jnp.float32),
            jnp.zeros((4, tile_rows, MAX_PICKED, key_tiles.shape[1]), jnp.float32),
        )
        running_max, running_sum, score_store = lax.fori_loop(0, head_count, statistics, initial)
        log_total = (running_max + jnp.log(running_sum))[..., None]

        def forward(column, running_out):
            blocks = lax.dynamic_index_in_dim(chosen, column, 1, keepdims=False)
            score_matrix = lax.dynamic_index_in_dim(score_store, column, 2, keepdims=False)
            value_tile = jnp.take(value_tiles, blocks, axis=0)
            weights = jnp.exp(score_matrix - log_total).astype(jnp.bfloat16)
            return running_out + jnp.einsum(
                "gqk,gkd->gqd", weights, value_tile, preferred_element_type=jnp.float32
            )

        output_tile = lax.fori_loop(
            0, head_count, forward, jnp.zeros((4, tile_rows, HEAD_WIDTH), jnp.float32)
        ).astype(jnp.bfloat16)
        row_delta = jnp.sum(
            grad_tile.astype(jnp.float32) * output_tile.astype(jnp.float32), axis=-1
        )[..., None]

        def backward(column, carried):
            query_total, key_sum, value_sum = carried
            blocks = lax.dynamic_index_in_dim(chosen, column, 1, keepdims=False)
            score_matrix = lax.dynamic_index_in_dim(score_store, column, 2, keepdims=False)
            key_tile = jnp.take(key_tiles, blocks, axis=0)
            value_tile = jnp.take(value_tiles, blocks, axis=0)
            weights = jnp.exp(score_matrix - log_total)
            weight_gradient = jnp.einsum(
                "gqd,gkd->gqk", grad_tile, value_tile, preferred_element_type=jnp.float32
            )
            score_gradient = (weights * (weight_gradient - row_delta) * softmax_scale).astype(
                jnp.bfloat16
            )
            query_total = query_total + jnp.einsum(
                "gqk,gkd->gqd", score_gradient, key_tile, preferred_element_type=jnp.float32
            )
            key_sum = key_sum.at[blocks].add(
                jnp.einsum(
                    "gqk,gqd->gkd", score_gradient, query_tile, preferred_element_type=jnp.float32
                )
            )
            value_sum = value_sum.at[blocks].add(
                jnp.einsum(
                    "gqk,gqd->gkd",
                    weights.astype(jnp.bfloat16),
                    grad_tile,
                    preferred_element_type=jnp.float32,
                )
            )
            return (query_total, key_sum, value_sum)

        initial_grads = (jnp.zeros((4, tile_rows, HEAD_WIDTH), jnp.float32), key_total, value_total)
        query_total, key_total, value_total = lax.fori_loop(0, head_count, backward, initial_grads)
        attended = lax.dynamic_update_slice_in_dim(attended, output_tile, group_step * 4, 0)
        query_gradient = lax.dynamic_update_slice_in_dim(
            query_gradient, query_total.astype(jnp.bfloat16), group_step * 4, 0
        )
        return (attended, query_gradient, key_total, value_total)

    blank = jnp.zeros(query_item.shape, jnp.bfloat16)
    return lax.fori_loop(0, group_count, one_group, (blank, blank, key_accum, value_accum))


def local(queries, keys, values, grad_out, layout, counts):
    context_size = lax.axis_size("context")
    context_rank = lax.axis_index("context")
    member = lax.axis_index("dp") % 2
    query_portions = max(1, context_size // QUERY_HEADS)
    holder_split = query_portions * QUERY_HEADS // context_size
    group_holders = QUERY_HEADS // KEY_VALUE_HEADS * query_portions // holder_split
    query_count = queries.shape[0]
    key_number = keys.shape[0]
    part_rows = query_count // query_portions
    kv_local = jnp.stack([keys, values])
    stacking_depth = kv_local.shape[0]
    query_in, grad_in, kv_in = (
        lax.all_to_all(
            owner_rows(queries, context_size, holder_split, query_portions),
            "context",
            split_axis=0,
            concat_axis=0,
            tiled=True,
        ),
        lax.all_to_all(
            owner_rows(grad_out, context_size, holder_split, query_portions),
            "context",
            split_axis=0,
            concat_axis=0,
            tiled=True,
        ),
        lax.all_to_all(
            head_pieces(kv_local, group_holders, context_size),
            "context",
            split_axis=0,
            concat_axis=0,
            tiled=True,
        ),
    )
    kv_half = kv_in.reshape(context_size, stacking_depth, key_number, HEAD_WIDTH).transpose(
        1, 0, 2, 3
    )
    kv_half = kv_half.reshape(stacking_depth, context_size * key_number, HEAD_WIDTH)
    partner_half = swapped(kv_half, "dp", 0)
    kv_full = in_order(kv_half, partner_half, member, 1)
    key_tiles = kv_full[0].reshape(-1, LAYOUT_BLOCK, HEAD_WIDTH)
    value_tiles = kv_full[1].reshape(-1, LAYOUT_BLOCK, HEAD_WIDTH)
    block_rows = context_size * part_rows // LAYOUT_BLOCK
    query_items = query_in.reshape(context_size, holder_split, part_rows, HEAD_WIDTH).transpose(
        1, 0, 2, 3
    )
    grad_items = grad_in.reshape(context_size, holder_split, part_rows, HEAD_WIDTH).transpose(
        1, 0, 2, 3
    )
    local_blocks = jnp.arange(block_rows, dtype=jnp.int32)
    part_blocks = part_rows // LAYOUT_BLOCK
    device_blocks = query_count // LAYOUT_BLOCK
    key_accum = jnp.zeros(key_tiles.shape, jnp.float32)
    value_accum = jnp.zeros(value_tiles.shape, jnp.float32)
    item_index = context_rank * holder_split + 0
    head_index = item_index // query_portions
    part_index = item_index % query_portions
    sequence_blocks = (
        member * context_size * device_blocks
        + local_blocks // part_blocks * device_blocks
        + part_index * part_blocks
        + local_blocks % part_blocks
    )
    head_layout = lax.dynamic_index_in_dim(layout, head_index, 0, keepdims=False)
    picked = jnp.take(head_layout, sequence_blocks, axis=0)
    head_count = lax.dynamic_index_in_dim(counts, head_index, 0, keepdims=False)
    attended_item, grad_item_out, key_accum, value_accum = attend_item(
        query_items[0],
        grad_items[0],
        picked,
        head_count,
        key_tiles,
        value_tiles,
        key_accum,
        value_accum,
    )
    output_rows = [attended_item]
    query_grads = [grad_item_out]

    def back_rows(tiles):
        stacked_rows = jnp.stack(tiles).transpose(1, 0, 2, 3)
        return stacked_rows.reshape(context_size, holder_split * part_rows, HEAD_WIDTH)

    out_back, grad_back = (
        lax.all_to_all(back_rows(output_rows), "context", split_axis=0, concat_axis=0, tiled=True),
        lax.all_to_all(back_rows(query_grads), "context", split_axis=0, concat_axis=0, tiled=True),
    )
    attended_rows = token_rows_back(out_back, query_portions)
    query_grad_rows = token_rows_back(grad_back, query_portions)
    grads_full = jnp.stack([key_accum, value_accum]).reshape(
        2, 2, context_size, key_number, HEAD_WIDTH
    )
    own_half = jnp.where(member == 0, grads_full[:, 0], grads_full[:, 1])
    other_half = jnp.where(member == 0, grads_full[:, 1], grads_full[:, 0])
    own_total = own_half + swapped(other_half.astype(jnp.bfloat16), "dp", 0).astype(
        other_half.dtype
    )
    grads_send = own_total.transpose(1, 0, 2, 3).reshape(context_size, 2 * key_number, HEAD_WIDTH)
    incoming_gradient = lax.all_to_all(
        grads_send.astype(jnp.bfloat16), "context", split_axis=0, concat_axis=0, tiled=True
    ).astype(grads_send.dtype)
    summed_rows = incoming_gradient.reshape(KEY_VALUE_HEADS, group_holders, -1, HEAD_WIDTH).sum(
        axis=1
    )
    merged_rows = summed_rows.reshape(KEY_VALUE_HEADS, 2, key_number, HEAD_WIDTH)
    key_gradient = (
        merged_rows[:, 0]
        .transpose(1, 0, 2)
        .reshape(key_number, KEY_VALUE_HEADS * HEAD_WIDTH)
        .astype(jnp.bfloat16)
    )
    value_gradient = (
        merged_rows[:, 1]
        .transpose(1, 0, 2)
        .reshape(key_number, KEY_VALUE_HEADS * HEAD_WIDTH)
        .astype(jnp.bfloat16)
    )
    return (attended_rows, query_grad_rows, key_gradient, value_gradient)


def solution(mesh):
    placed = (
        P(("dp", "context"), None),
        P(("dp", "context"), None),
        P(("dp", "context"), None),
        P(("dp", "context"), None),
        P(),
        P(),
    )
    return jax.shard_map(
        local,
        mesh=mesh,
        in_specs=placed,
        out_specs=(
            P(("dp", "context"), None),
            P(("dp", "context"), None),
            P(("dp", "context"), None),
            P(("dp", "context"), None),
        ),
        check_vma=False,
    )
```

profile of v0, /device:TPU:1, one launch (start us, length us, event | category | flops | bytes accessed | tf_op | source)
XLA Modules:
  0.0 851.4 jit_solution(16336921344650694064)
XLA Ops:
  3.8 16.7 %all-to-all-start.1 = ((bf16[32,128,128]{2,1,0:T(8,128)(2,1)}), bf16[32,128,128]{2,1,0:T(8,128)(2,1)S(1)}, u32[]{:S(2)}, u32[]{:S(2)}) async-start(bf16[32,128,128]{2,1,0:T(8,128)(2,1)} %bitcast.20), calls=%async_computation.1 | async-start | bytes 2097152 | tf_op jit(solution)/shard_map/all_to_all | solution.py:180
  22.1 54.2 %all-to-all-done.1 = bf16[32,128,128]{2,1,0:T(8,128)(2,1)S(1)} async-done(((bf16[32,128,128]{2,1,0:T(8,128)(2,1)}), bf16[32,128,128]{2,1,0:T(8,128)(2,1)S(1)}, u32[]{:S(2)}, u32[]{:S(2)}) %all-to-all-start.1) | async-done | bytes 1048608 | tf_op jit(solution)/shard_map/all_to_all | solution.py:180
  76.3 4.8 all-to-all-start
  82.5 54.3 %all-to-all-done = bf16[32,128,128]{2,1,0:T(8,128)(2,1)} async-done(((bf16[32,128,128]{2,1,0:T(8,128)(2,1)}), bf16[32,128,128]{2,1,0:T(8,128)(2,1)}, u32[]{:S(2)}, u32[]{:S(2)}) %all-to-all-start) | async-done | bytes 1048608 | tf_op jit(solution)/shard_map/all_to_all | solution.py:166
  136.9 5.4 all-to-all-start.2
  142.4 3.1 collective-permute-start
  147.0 21.7 %collective-permute-done = bf16[2,2048,128]{2,1,0:T(8,128)(2,1)S(1)} collective-permute-done((bf16[2,2048,128]{2,1,0:T(8,128)(2,1)S(1)}, bf16[2,2048,128]{2,1,0:T(8,128)(2,1)S(1)}, u32[]{:S(2)}, u32[]{:S(2)}) %collective-permute-start) | collective-permute-done | bytes 1048608 | tf_op jit(solution)/shard_map/ppermute | solution.py:22
  170.4 27.8 %all-to-all-done.2 = bf16[32,128,128]{2,1,0:T(8,128)(2,1)} async-done(((bf16[32,128,128]{2,1,0:T(8,128)(2,1)}), bf16[32,128,128]{2,1,0:T(8,128)(2,1)}, u32[]{:S(2)}, u32[]{:S(2)}) %all-to-all-start.2) | async-done | bytes 1048608 | tf_op jit(solution)/shard_map/all_to_all | solution.py:173
  203.7 464.6 %while.108 = (s32[]{:T(128)}, bf16[32,128,128]{2,1,0:T(8,128)(2,1)}, bf16[32,128,128]{2,1,0:T(8,128)(2,1)}, f32[32,128,128]{2,1,0:T(8,128)}, f32[32,128,128]{2,1...) while((s32[]{:T(128)}, bf16[32,128,128]{2,1,0:T(8,128)(2,1)}, ...), condition=%wide.region_12.14_spmd, body=%wide.region_0.13_spmd.sunk | while | flops 102502496 | bytes 11726504 | solution.py:150
  204.9 12.2 %while.109 = (s32[]{:T(128)}, f32[4,128]{1,0:T(4,128)S(1)}, f32[4,128]{1,0:T(4,128)S(1)}, f32[4,128,4,128]{1,3,0,2:T(8,128)S(1)}, s32[]{:T(128)}, /*index=5*/s32...) while((s32[]{:T(128)}, f32[4,128]{1,0:T(4,128)S(1)}, ...), condition=%wide.region_4.5_spmd, body=%wide.region_1.4_spmd.sunk | while | flops 17106972 | bytes 1603815 | solution.py:91
  217.1 7.6 while.110
  225.9 35.1 %while.111 = (s32[]{:T(128)}, f32[4,128,128]{2,1,0:T(8,128)S(1)}, f32[32,128,128]{2,1,0:T(8,128)}, f32[32,128,128]{2,1,0:T(8,128)}, s32[]{:T(128)}, /*index=5*/f...) while((s32[]{:T(128)}, f32[4,128,128]{2,1,0:T(8,128)S(1)}, ...), condition=%wide.region_11.12_spmd, body=%wide.region_8.11_spmd.sunk | while | flops 67896360 | bytes 4729195 | solution.py:142
  257.9 2.3 scatter_fusion
  262.8 12.2 %while.109 = (s32[]{:T(128)}, f32[4,128]{1,0:T(4,128)S(1)}, f32[4,128]{1,0:T(4,128)S(1)}, f32[4,128,4,128]{1,3,0,2:T(8,128)S(1)}, s32[]{:T(128)}, /*index=5*/s32...) while((s32[]{:T(128)}, f32[4,128]{1,0:T(4,128)S(1)}, ...), condition=%wide.region_4.5_spmd, body=%wide.region_1.4_spmd.sunk | while | flops 17106972 | bytes 1603815 | solution.py:91
  275.1 7.6 while.110
  283.8 35.2 %while.111 = (s32[]{:T(128)}, f32[4,128,128]{2,1,0:T(8,128)S(1)}, f32[32,128,128]{2,1,0:T(8,128)}, f32[32,128,128]{2,1,0:T(8,128)}, s32[]{:T(128)}, /*index=5*/f...) while((s32[]{:T(128)}, f32[4,128,128]{2,1,0:T(8,128)S(1)}, ...), condition=%wide.region_11.12_spmd, body=%wide.region_8.11_spmd.sunk | while | flops 67896360 | bytes 4729195 | solution.py:142
  287.9 2.3 scatter_fusion.1
  320.9 12.2 %while.109 = (s32[]{:T(128)}, f32[4,128]{1,0:T(4,128)S(1)}, f32[4,128]{1,0:T(4,128)S(1)}, f32[4,128,4,128]{1,3,0,2:T(8,128)S(1)}, s32[]{:T(128)}, /*index=5*/s32...) while((s32[]{:T(128)}, f32[4,128]{1,0:T(4,128)S(1)}, ...), condition=%wide.region_4.5_spmd, body=%wide.region_1.4_spmd.sunk | while | flops 17106972 | bytes 1603815 | solution.py:91
  333.2 7.6 while.110
  341.9 35.2 %while.111 = (s32[]{:T(128)}, f32[4,128,128]{2,1,0:T(8,128)S(1)}, f32[32,128,128]{2,1,0:T(8,128)}, f32[32,128,128]{2,1,0:T(8,128)}, s32[]{:T(128)}, /*index=5*/f...) while((s32[]{:T(128)}, f32[4,128,128]{2,1,0:T(8,128)S(1)}, ...), condition=%wide.region_11.12_spmd, body=%wide.region_8.11_spmd.sunk | while | flops 67896360 | bytes 4729195 | solution.py:142
  379.0 12.2 %while.109 = (s32[]{:T(128)}, f32[4,128]{1,0:T(4,128)S(1)}, f32[4,128]{1,0:T(4,128)S(1)}, f32[4,128,4,128]{1,3,0,2:T(8,128)S(1)}, s32[]{:T(128)}, /*index=5*/s32...) while((s32[]{:T(128)}, f32[4,128]{1,0:T(4,128)S(1)}, ...), condition=%wide.region_4.5_spmd, body=%wide.region_1.4_spmd.sunk | while | flops 17106972 | bytes 1603815 | solution.py:91
  391.3 7.6 while.110
  400.0 35.2 %while.111 = (s32[]{:T(128)}, f32[4,128,128]{2,1,0:T(8,128)S(1)}, f32[32,128,128]{2,1,0:T(8,128)}, f32[32,128,128]{2,1,0:T(8,128)}, s32[]{:T(128)}, /*index=5*/f...) while((s32[]{:T(128)}, f32[4,128,128]{2,1,0:T(8,128)S(1)}, ...), condition=%wide.region_11.12_spmd, body=%wide.region_8.11_spmd.sunk | while | flops 67896360 | bytes 4729195 | solution.py:142
  414.9 2.3 scatter_fusion
  437.1 12.2 %while.109 = (s32[]{:T(128)}, f32[4,128]{1,0:T(4,128)S(1)}, f32[4,128]{1,0:T(4,128)S(1)}, f32[4,128,4,128]{1,3,0,2:T(8,128)S(1)}, s32[]{:T(128)}, /*index=5*/s32...) while((s32[]{:T(128)}, f32[4,128]{1,0:T(4,128)S(1)}, ...), condition=%wide.region_4.5_spmd, body=%wide.region_1.4_spmd.sunk | while | flops 17106972 | bytes 1603815 | solution.py:91
  449.4 7.6 while.110
  458.1 35.2 %while.111 = (s32[]{:T(128)}, f32[4,128,128]{2,1,0:T(8,128)S(1)}, f32[32,128,128]{2,1,0:T(8,128)}, f32[32,128,128]{2,1,0:T(8,128)}, s32[]{:T(128)}, /*index=5*/f...) while((s32[]{:T(128)}, f32[4,128,128]{2,1,0:T(8,128)S(1)}, ...), condition=%wide.region_11.12_spmd, body=%wide.region_8.11_spmd.sunk | while | flops 67896360 | bytes 4729195 | solution.py:142
  464.4 2.3 scatter_fusion
  495.2 12.2 %while.109 = (s32[]{:T(128)}, f32[4,128]{1,0:T(4,128)S(1)}, f32[4,128]{1,0:T(4,128)S(1)}, f32[4,128,4,128]{1,3,0,2:T(8,128)S(1)}, s32[]{:T(128)}, /*index=5*/s32...) while((s32[]{:T(128)}, f32[4,128]{1,0:T(4,128)S(1)}, ...), condition=%wide.region_4.5_spmd, body=%wide.region_1.4_spmd.sunk | while | flops 17106972 | bytes 1603815 | solution.py:91
  507.5 7.6 while.110
  516.2 35.2 %while.111 = (s32[]{:T(128)}, f32[4,128,128]{2,1,0:T(8,128)S(1)}, f32[32,128,128]{2,1,0:T(8,128)}, f32[32,128,128]{2,1,0:T(8,128)}, s32[]{:T(128)}, /*index=5*/f...) while((s32[]{:T(128)}, f32[4,128,128]{2,1,0:T(8,128)S(1)}, ...), condition=%wide.region_11.12_spmd, body=%wide.region_8.11_spmd.sunk | while | flops 67896360 | bytes 4729195 | solution.py:142
  553.2 12.2 %while.109 = (s32[]{:T(128)}, f32[4,128]{1,0:T(4,128)S(1)}, f32[4,128]{1,0:T(4,128)S(1)}, f32[4,128,4,128]{1,3,0,2:T(8,128)S(1)}, s32[]{:T(128)}, /*index=5*/s32...) while((s32[]{:T(128)}, f32[4,128]{1,0:T(4,128)S(1)}, ...), condition=%wide.region_4.5_spmd, body=%wide.region_1.4_spmd.sunk | while | flops 17106972 | bytes 1603815 | solution.py:91
  565.5 7.6 while.110
  574.2 35.2 %while.111 = (s32[]{:T(128)}, f32[4,128,128]{2,1,0:T(8,128)S(1)}, f32[32,128,128]{2,1,0:T(8,128)}, f32[32,128,128]{2,1,0:T(8,128)}, s32[]{:T(128)}, /*index=5*/f...) while((s32[]{:T(128)}, f32[4,128,128]{2,1,0:T(8,128)S(1)}, ...), condition=%wide.region_11.12_spmd, body=%wide.region_8.11_spmd.sunk | while | flops 67896360 | bytes 4729195 | solution.py:142
  578.2 2.3 scatter_fusion.1
  586.9 2.3 scatter_fusion.1
  606.5 2.4 scatter_fusion
  611.4 12.2 %while.109 = (s32[]{:T(128)}, f32[4,128]{1,0:T(4,128)S(1)}, f32[4,128]{1,0:T(4,128)S(1)}, f32[4,128,4,128]{1,3,0,2:T(8,128)S(1)}, s32[]{:T(128)}, /*index=5*/s32...) while((s32[]{:T(128)}, f32[4,128]{1,0:T(4,128)S(1)}, ...), condition=%wide.region_4.5_spmd, body=%wide.region_1.4_spmd.sunk | while | flops 17106972 | bytes 1603815 | solution.py:91
  623.6 7.6 while.110
  632.4 35.2 %while.111 = (s32[]{:T(128)}, f32[4,128,128]{2,1,0:T(8,128)S(1)}, f32[32,128,128]{2,1,0:T(8,128)}, f32[32,128,128]{2,1,0:T(8,128)}, s32[]{:T(128)}, /*index=5*/f...) while((s32[]{:T(128)}, f32[4,128,128]{2,1,0:T(8,128)S(1)}, ...), condition=%wide.region_11.12_spmd, body=%wide.region_8.11_spmd.sunk | while | flops 67896360 | bytes 4729195 | solution.py:142
  655.9 2.3 scatter_fusion
  668.3 60.7 %all_to_all.30 = bf16[32,128,128]{2,1,0:T(8,128)(2,1)S(1)} all-to-all(bf16[32,128,128]{2,1,0:T(8,128)(2,1)} %get-tuple-element.349), channel_id=1, replica_groups=mesh['dp'=16,'context'=32] {'context'}, dimensions={0} | all-to-all | bytes 2097152 | tf_op jit(solution)/shard_map/all_to_all | solution.py:238
  729.0 5.3 all-to-all-start.4
  736.3 2.9 collective-permute-start.1
  739.2 23.4 %collective-permute-done.1 = bf16[2,32,64,128]{3,2,0,1:T(8,128)(2,1)S(1)} collective-permute-done((bf16[2,32,64,128]{3,2,0,1:T(8,128)(2,1)S(1)}, bf16[2,32,64,128]{3,2,0,1:T(8,128)(2,1)S(1)}, u32[]{:S(2)}, u32[]{:S(2)}) %collective-permute-start.1) | collective-permute-done | bytes 1048608 | tf_op jit(solution)/shard_map/ppermute | solution.py:22
  764.1 26.0 %all-to-all-done.4 = bf16[32,128,128]{2,1,0:T(8,128)(2,1)} async-done(((bf16[32,128,128]{2,1,0:T(8,128)(2,1)}), bf16[32,128,128]{2,1,0:T(8,128)(2,1)}, u32[]{:S(2)}, u32[]{:S(2)}) %all-to-all-start.4) | async-done | bytes 1048608 | tf_op jit(solution)/shard_map/all_to_all | solution.py:239
  790.2 4.6 all-to-all-start.5
  799.2 51.4 %all-to-all-done.5 = bf16[32,128,128]{2,1,0:T(8,128)(2,1)S(1)} async-done(((bf16[32,128,128]{2,1,0:T(8,128)(2,1)}), bf16[32,128,128]{2,1,0:T(8,128)(2,1)S(1)}, u32[]{:S(2)}, u32[]{:S(2)}) %all-to-all-start.5) | async-done | bytes 1048608 | tf_op jit(solution)/shard_map/all_to_all | solution.py:252
  (956 shorter events, 384.4 us)
Async XLA Ops:
  0.6 145.5 %copy-start = (s32[16,128,4]{1,2,0:T(4,128)S(1)}, s32[16,128,4]{1,2,0:T(4,128)}, u32[]{:S(2)}) copy-start(s32[16,128,4]{1,2,0:T(4,128)} %param.20) | copy-start | bytes 98308
  0.6 19.9 %copy-start.3 = (bf16[256,2048]{1,0:T(8,128)(2,1)S(1)}, bf16[256,2048]{1,0:T(8,128)(2,1)}, u32[]{:S(2)}) copy-start(bf16[256,2048]{1,0:T(8,128)(2,1)} %param.16) | copy-start | bytes 3145732
  3.8 72.4 %all-to-all-start.1 = ((bf16[32,128,128]{2,1,0:T(8,128)(2,1)}), bf16[32,128,128]{2,1,0:T(8,128)(2,1)S(1)}, u32[]{:S(2)}, u32[]{:S(2)}) async-start(bf16[32,128,128]{2,1,0:T(8,128)(2,1)} %bitcast.20), calls=%async_computation.1 | async-start | bytes 2097152 | tf_op jit(solution)/shard_map/all_to_all | solution.py:180
  20.8 60.2 %copy-start.4 = (bf16[256,2048]{1,0:T(8,128)(2,1)S(1)}, bf16[256,2048]{1,0:T(8,128)(2,1)}, u32[]{:S(2)}) copy-start(bf16[256,2048]{1,0:T(8,128)(2,1)} %param.19) | copy-start | bytes 3145732
  76.3 60.6 %all-to-all-start = ((bf16[32,128,128]{2,1,0:T(8,128)(2,1)}), bf16[32,128,128]{2,1,0:T(8,128)(2,1)}, u32[]{:S(2)}, u32[]{:S(2)}) async-start(bf16[32,128,128]{2,1,0:T(8,128)(2,1)} %bitcast.17), calls=%async_computation | async-start | bytes 2097152 | tf_op jit(solution)/shard_map/all_to_all | solution.py:166
  136.9 8.7 %copy-start.5 = (s32[16]{0:T(128)S(1)}, s32[16]{0:T(128)}, u32[]{:S(2)}) copy-start(s32[16]{0:T(128)} %param.21) | copy-start | bytes 196
  136.9 61.3 %all-to-all-start.2 = ((bf16[32,128,128]{2,1,0:T(8,128)(2,1)}), bf16[32,128,128]{2,1,0:T(8,128)(2,1)}, u32[]{:S(2)}, u32[]{:S(2)}) async-start(bf16[32,128,128]{2,1,0:T(8,128)(2,1)} %bitcast.27), calls=%async_computation.2 | async-start | bytes 2097152 | tf_op jit(solution)/shard_map/all_to_all | solution.py:173
  142.4 26.3 %collective-permute-start = (bf16[2,2048,128]{2,1,0:T(8,128)(2,1)S(1)}, bf16[2,2048,128]{2,1,0:T(8,128)(2,1)S(1)}, u32[]{:S(2)}, u32[]{:S(2)}) collective-permute-start(bf16[2,2048,128]{2,1,0:T(8,128)(2,1)S(1)} %bitcast.169), channel_id=1, source_target_pairs={{0,32},{32,0},{64,96},{96,64},{128,160},{160,128},{192,224},{224,1... | collective-permute-start | bytes 3145736 | tf_op jit(solution)/shard_map/ppermute | solution.py:22
  668.3 66.0 %copy-start.1 = (f32[32,128,128]{2,1,0:T(8,128)S(1)}, f32[32,128,128]{2,1,0:T(8,128)}, u32[]{:S(2)}) copy-start(f32[32,128,128]{2,1,0:T(8,128)} %get-tuple-element.352) | copy-start | bytes 6291460
  729.0 61.1 %all-to-all-start.4 = ((bf16[32,128,128]{2,1,0:T(8,128)(2,1)}), bf16[32,128,128]{2,1,0:T(8,128)(2,1)}, u32[]{:S(2)}, u32[]{:S(2)}) async-start(bf16[32,128,128]{2,1,0:T(8,128)(2,1)} %get-tuple-element.350), calls=%async_computation.4 | async-start | bytes 2097152 | tf_op jit(solution)/shard_map/all_to_all | solution.py:239
  734.3 28.2 %copy-start.2 = (f32[32,128,128]{2,1,0:T(8,128)S(1)}, f32[32,128,128]{2,1,0:T(8,128)}, u32[]{:S(2)}) copy-start(f32[32,128,128]{2,1,0:T(8,128)} %get-tuple-element.351) | copy-start | bytes 6291460
  736.3 26.3 %collective-permute-start.1 = (bf16[2,32,64,128]{3,2,0,1:T(8,128)(2,1)S(1)}, bf16[2,32,64,128]{3,2,0,1:T(8,128)(2,1)S(1)}, u32[]{:S(2)}, u32[]{:S(2)}) collective-permute-start(bf16[2,32,64,128]{3,2,0,1:T(8,128)(2,1)S(1)} %fusion.35), channel_id=1, source_target_pairs={{0,32},{32,0},{64,96},{96,64},{128,160},{160,128},{192,224},{224,1... | collective-permute-start | bytes 3145736 | tf_op jit(solution)/shard_map/ppermute | solution.py:22
  790.2 60.4 %all-to-all-start.5 = ((bf16[32,128,128]{2,1,0:T(8,128)(2,1)}), bf16[32,128,128]{2,1,0:T(8,128)(2,1)S(1)}, u32[]{:S(2)}, u32[]{:S(2)}) async-start(bf16[32,128,128]{2,1,0:T(8,128)(2,1)} %bitcast.37), calls=%async_computation.5 | async-start | bytes 2097152 | tf_op jit(solution)/shard_map/all_to_all | solution.py:252
where the time goes:
time: 859 us; the launch traced here: 851 us
  waiting for transfers between devices  259 us (30%)
  local copies, waits for them, and re-layouts  186 us (22%)
  other arithmetic  171 us (20%)
  loops' own time  85 us (10%)
  blocking collectives  60.7 us (7%)
  matrix products  45.9 us (5%)
  starting transfers between devices  42.9 us (5%)
    scatter-add x32, other arithmetic, backward(): key_sum.at[blocks]  74 us
    scatter-add x32, other arithmetic, backward(): value_sum.at[blocks]  73.9 us
    all_to_all x1, blocking collectives, local(): lax.all_to_all(back_rows(output_rows), 'context', split_axis=0, concat_ax...  60.7 us
    gather x32, local copies, waits for them, and re-layouts, backward(): key_tile = jnp.take(key_tiles, blocks, axis=0)  57.5 us
    gather x32, local copies, waits for them, and re-layouts, statistics(): key_tile = jnp.take(key_tiles, blocks, axis=0)  57.5 us
    all_to_all x1, waiting for transfers between devices, local(): lax.all_to_all(owner_rows(queries, context_size, holder_split, query_port...  54.3 us
    all_to_all x1, waiting for transfers between devices, local(): lax.all_to_all(head_pieces(kv_local, group_holders, context_size), 'conte...  54.2 us
    all_to_all x1, waiting for transfers between devices, local(): lax.all_to_all(grads_send.astype(jnp.bfloat16), 'context', split_axis=0,...  51.4 us
  transfers between devices with their start and end apart: 7, of which 7 were waited for; matrix products, arithmetic and copies ran while one was open for 2% of the time, Pallas kernels for 0%

commit v1 on v0

v1 whole, which is shorter than its diff:
```python
import functools
import math

import jax
import jax.numpy as jnp
from jax import lax
from jax.experimental import pallas as pl
from jax.experimental.pallas import tpu as pltpu
from jax.sharding import PartitionSpec as P

QUERY_HEADS = 16
KEY_VALUE_HEADS = 4
HEAD_WIDTH = 128
BLOCK = 128
GROUP_WIDTH = 4 * HEAD_WIDTH
MESH = pl.DeviceIdType.MESH
VMEM_SPEC = pl.BlockSpec(memory_space=pltpu.VMEM)
ANY_SPEC = pl.BlockSpec(memory_space=pl.ANY)
SCALE = 1.0 / math.sqrt(HEAD_WIDTH)
SCALE_LOG2E = SCALE / math.log(2.0)
ROUTES = ((0, 0), (0, 1), (1, 0), (1, 1))


class Place:
    def __init__(self, ring):
        dp = lax.axis_index("dp")
        context = lax.axis_index("context")
        self.ring = ring
        self.dp = dp
        self.member = dp % 2
        self.core = context % 2
        self.z = context // 2
        self.head = self.member * 2 + self.core

    def partner(self, route):
        flip_member, flip_core = route
        member = 1 - self.member if flip_member else self.member
        core = 1 - self.core if flip_core else self.core
        return member, core, member * 2 + core, (self.dp - self.member + member, self.z * 2 + core)

    def ring_device(self, step):
        return (self.dp, (self.z + step + self.ring) % self.ring * 2 + self.core)

    def enter(self):
        barrier = pltpu.get_barrier_semaphore()
        others = [self.partner(route)[3] for route in ROUTES[1:]]
        others += [self.ring_device(1), self.ring_device(-1)]
        for other in others:
            pl.semaphore_signal(barrier, inc=1, device_id=other, device_id_type=MESH)
        pl.semaphore_wait(barrier, len(others))


def columns(index, width):
    return pl.ds(pl.multiple_of(index * width, width), width)


def gather_kernel(
    ring, q, g, k, v, qg, gg, kf, vf, own_sem, send_x, recv_x, send_z, recv_z
):
    place = Place(ring)
    place.enter()
    half = k.shape[0]
    own_block = place.member * ring + place.z
    small, large = [], []
    for t, (source, target) in enumerate(((k, kf), (v, vf), (q, qg), (g, gg))):
        copies = small if t < 2 else large
        width = HEAD_WIDTH if t < 2 else GROUP_WIDTH
        if t < 2:
            landing = target.at[own_block, columns(place.core, half), :]
        else:
            landing = target.at[place.head]
        for i, route in enumerate(ROUTES):
            _, _, head, device = place.partner(route)
            piece = source.at[:, columns(head, width)]
            if i == 0:
                copy = pltpu.make_async_copy(piece, landing, own_sem.at[t])
            else:
                copy = pltpu.make_async_remote_copy(
                    src_ref=piece,
                    dst_ref=landing,
                    send_sem=send_x.at[t, i - 1],
                    recv_sem=recv_x.at[t, i - 1],
                    device_id=device,
                    device_id_type=MESH,
                )
            copies.append((i, copy))
            copy.start()
    for i, copy in small:
        copy.wait() if i == 0 else copy.wait_recv()

    def hop(way, chunk, slot, sub):
        buffer = (kf, vf)[sub // 2]
        sign = 1 if way == 0 else -1
        block = sub % 2 * ring + (place.z - sign * chunk + ring) % ring
        return pltpu.make_async_remote_copy(
            src_ref=buffer.at[block],
            dst_ref=buffer.at[block],
            send_sem=send_z.at[way, slot, sub],
            recv_sem=recv_z.at[way, slot, sub],
            device_id=place.ring_device(sign),
            device_id_type=MESH,
        )

    pairs = [(way, sub) for sub in range(4) for way in range(2)]
    last = [(0, 0), (1, 2), (0, 1), (1, 3)]
    far = ring // 2
    for way, sub in pairs:
        hop(way, 0, 0, sub).start()

    def forward(step, carry):
        for way, sub in pairs:
            hop(way, step, step - 1, sub).wait_recv()
            hop(way, step, step, sub).start()
        return carry

    lax.fori_loop(1, far - 1, forward, 0)
    for way, sub in pairs:
        hop(way, far - 1, far - 2, sub).wait_recv()
        if (way, sub) in last:
            hop(way, far - 1, far - 1, sub).start()
    for way, sub in last:
        hop(way, far, far - 1, sub).wait_recv()

    def drain(step, carry):
        for way, sub in pairs:
            hop(way, step, step, sub).wait_send()
        return carry

    lax.fori_loop(0, far - 1, drain, 0)
    for way, sub in last:
        hop(way, far - 1, far - 1, sub).wait_send()
    for i, copy in small:
        if i > 0:
            copy.wait_send()
    for i, copy in large:
        copy.wait()


def scatter_kernel(
    ring, o, dq, dk, dv, att, dqo, dko, dvo, landed, final, own_sem, send_x, recv_x, send_z, recv_z
):
    place = Place(ring)
    place.enter()
    half = dko.shape[0]
    copies = []

    def exchange(t, source, target, width):
        for i, route in enumerate(ROUTES):
            member, core, head, device = place.partner(route)
            piece = source(member, core, head)
            landing = target.at[:, columns(place.head, width)]
            if i == 0:
                copy = pltpu.make_async_copy(piece, landing, own_sem.at[t])
            else:
                copy = pltpu.make_async_remote_copy(
                    src_ref=piece,
                    dst_ref=landing,
                    send_sem=send_x.at[t, i - 1],
                    recv_sem=recv_x.at[t, i - 1],
                    device_id=device,
                    device_id_type=MESH,
                )
            copies.append(copy)
            copy.start()

    far = ring // 2

    def partial(sub, way, distance):
        sign = 1 if way == 0 else -1
        block = sub % 2 * ring + (place.z + sign * distance + ring) % ring
        return (dk, dv)[sub // 2].at[block]

    def hop(source, way, slot, sub):
        return pltpu.make_async_remote_copy(
            src_ref=source,
            dst_ref=landed.at[way, slot, sub],
            send_sem=send_z.at[way, slot, sub],
            recv_sem=recv_z.at[way, slot, sub],
            device_id=place.ring_device(1 if way == 0 else -1),
            device_id_type=MESH,
        )

    def pass_on(way, distance, sub):
        slot = landed.at[way, distance, sub]
        hop(slot, way, distance, sub).wait_recv()
        slot[...] = (
            slot[...].astype(jnp.float32) + partial(sub, way, distance)[...].astype(jnp.float32)
        ).astype(jnp.bfloat16)
        hop(slot, way, distance - 1, sub).start()

    pairs = [(way, sub) for sub in range(4) for way in range(2)]
    longer = [(0, 0), (1, 2), (0, 1), (1, 3)]
    shorter = [pair for pair in pairs if pair not in longer]
    for way, sub in longer:
        hop(partial(sub, way, far), way, far - 1, sub).start()
    for way, sub in shorter:
        hop(partial(sub, way, far - 1), way, far - 2, sub).start()
    exchange(0, lambda member, core, head: o.at[head], att, GROUP_WIDTH)
    exchange(1, lambda member, core, head: dq.at[head], dqo, GROUP_WIDTH)
    for way, sub in longer:
        pass_on(way, far - 1, sub)

    def steps(i, carry):
        for way, sub in longer + shorter:
            pass_on(way, far - 2 - i, sub)
        return carry

    lax.fori_loop(0, far - 2, steps, 0)
    for sub in range(4):
        for way in range(2):
            hop(landed.at[way, 0, sub], way, 0, sub).wait_recv()
        total = (
            landed[0, 0, sub].astype(jnp.float32)
            + landed[1, 0, sub].astype(jnp.float32)
            + partial(sub, 0, 0)[...].astype(jnp.float32)
        )
        if sub < 2:
            total = total * SCALE
        final[sub] = total.astype(jnp.bfloat16)
    exchange(2, lambda member, core, head: final.at[member, columns(core, half), :], dko, HEAD_WIDTH)
    exchange(
        3, lambda member, core, head: final.at[2 + member, columns(core, half), :], dvo, HEAD_WIDTH
    )

    def drain(step, carry):
        for way, sub in pairs:
            hop(landed.at[way, step, sub], way, step, sub).wait_send()
        return carry

    lax.fori_loop(0, far - 1, drain, 0)
    for way, sub in longer:
        hop(landed.at[way, far - 1, sub], way, far - 1, sub).wait_send()
    for copy in copies:
        copy.wait()


def attend(count, unroll, z_blocks, head, start, q, g, k, v, kt, vt, o, dq, dka, dva, picked):
    lanes = columns(head, HEAD_WIDTH)
    nt = (((1,), (1,)), ((), ()))
    results = []
    for u in range(unroll):
        qi = start + u
        block = qi // 4 * (z_blocks * 4) + qi % 4
        chosen = [picked(head, j, block) for j in range(count)]
        query = q[qi, :, lanes]
        grad = g[qi, :, lanes]
        scores = lax.dot_general(
            jnp.concatenate([k[b] for b in chosen], 0), query, nt, preferred_element_type=jnp.float32
        )
        dweights = lax.dot_general(
            jnp.concatenate([v[b] for b in chosen], 0), grad, nt, preferred_element_type=jnp.float32
        )
        peak = jnp.max(scores, axis=0, keepdims=True)
        powers = jnp.exp2((scores - peak) * SCALE_LOG2E)
        weights = powers * (1.0 / jnp.sum(powers, axis=0, keepdims=True))
        delta = jnp.sum(weights * dweights, axis=0, keepdims=True)
        dscores = (weights * (dweights - delta)).astype(jnp.bfloat16)
        weights = weights.astype(jnp.bfloat16)
        out = jnp.dot(
            jnp.concatenate([vt[b] for b in chosen], 1), weights, preferred_element_type=jnp.float32
        )
        o[qi, :, lanes] = out.T.astype(jnp.bfloat16)
        dquery = jnp.dot(
            jnp.concatenate([kt[b] for b in chosen], 1), dscores, preferred_element_type=jnp.float32
        )
        dq[qi, :, lanes] = (dquery.T * SCALE).astype(jnp.bfloat16)
        dkey = jnp.dot(dscores, query, preferred_element_type=jnp.float32)
        dvalue = jnp.dot(weights, grad, preferred_element_type=jnp.float32)
        results.append((chosen, dkey, dvalue))
    for chosen, dkey, dvalue in results:
        for j, b in enumerate(chosen):
            rows = slice(j * BLOCK, (j + 1) * BLOCK)
            dka[b] += dkey[rows]
            dva[b] += dvalue[rows]


def attention_kernel(
    ring, unroll, lists, counts, q, g, k, v, o, dq, dk, dv, dka, dva, kt, vt, own_lists, sem
):
    place = Place(ring)
    copy = pltpu.make_async_copy(lists.at[pl.ds(place.head * 4, 4)], own_lists, sem)
    copy.start()
    blocks = k.shape[0]

    @pl.loop(0, blocks)
    def _(b):
        kt[b] = k[b].T
        vt[b] = v[b].T
        dka[b] = jnp.zeros((BLOCK, HEAD_WIDTH), jnp.float32)
        dva[b] = jnp.zeros((BLOCK, HEAD_WIDTH), jnp.float32)

    copy.wait()

    def picked(head, j, block):
        return own_lists[head, j, place.z * 4 + block]

    @pl.loop(0, 4)
    def _(head):
        used = counts[place.head * 4 + head]
        for count in range(1, 5):

            @pl.when(used == count)
            def _():
                @pl.loop(0, 8, step=unroll)
                def _(start):
                    attend(
                        count, unroll, ring, head, start, q, g, k, v, kt, vt, o, dq, dka, dva, picked
                    )

    @pl.loop(0, blocks)
    def _(b):
        dk[b] = dka[b].astype(jnp.bfloat16)
        dv[b] = dva[b].astype(jnp.bfloat16)


def attention(ring, lists, counts, qg, gg, kf, vf, unroll=2):
    tokens = jax.ShapeDtypeStruct((8, BLOCK, GROUP_WIDTH), jnp.bfloat16)
    rows = jax.ShapeDtypeStruct(kf.shape, jnp.bfloat16)
    return pl.pallas_call(
        functools.partial(attention_kernel, ring, unroll),
        out_shape=(tokens, tokens, rows, rows),
        in_specs=[ANY_SPEC, pl.BlockSpec(memory_space=pltpu.SMEM)] + [VMEM_SPEC] * 4,
        out_specs=(VMEM_SPEC,) * 4,
        scratch_shapes=[
            pltpu.VMEM(kf.shape, jnp.float32),
            pltpu.VMEM(kf.shape, jnp.float32),
            pltpu.VMEM(kf.shape, jnp.bfloat16),
            pltpu.VMEM(kf.shape, jnp.bfloat16),
            pltpu.SMEM((4, 4, lists.shape[2]), jnp.int32),
            pltpu.SemaphoreType.DMA,
        ],
        compiler_params=pltpu.CompilerParams(vmem_limit_bytes=40 << 20),
        name="attention",
    )(lists, counts, qg, gg, kf, vf)


def link_semaphores(ring):
    return [
        pltpu.SemaphoreType.DMA((4,)),
        pltpu.SemaphoreType.DMA((4, 3)),
        pltpu.SemaphoreType.DMA((4, 3)),
        pltpu.SemaphoreType.DMA((2, ring // 2, 4)),
        pltpu.SemaphoreType.DMA((2, ring // 2, 4)),
    ]


def local(queries, keys, values, grad_out, layout, counts):
    ring = lax.axis_size("context") // 2
    tokens = jax.ShapeDtypeStruct((4, queries.shape[0], GROUP_WIDTH), jnp.bfloat16)
    rows = jax.ShapeDtypeStruct((2 * ring, BLOCK, HEAD_WIDTH), jnp.bfloat16)
    qg, gg, kf, vf = pl.pallas_call(
        functools.partial(gather_kernel, ring),
        out_shape=(tokens, tokens, rows, rows),
        in_specs=[ANY_SPEC, ANY_SPEC, VMEM_SPEC, VMEM_SPEC],
        out_specs=(VMEM_SPEC,) * 4,
        scratch_shapes=link_semaphores(ring),
        compiler_params=pltpu.CompilerParams(
            collective_id=0, has_side_effects=True, vmem_limit_bytes=24 << 20
        ),
        name="gather",
    )(queries, grad_out, keys, values)
    shape = (8, BLOCK, GROUP_WIDTH)
    o, dq, dk, dv = attention(
        ring, layout.transpose(0, 2, 1), counts, qg.reshape(shape), gg.reshape(shape), kf, vf
    )
    return pl.pallas_call(
        functools.partial(scatter_kernel, ring),
        out_shape=tuple(
            jax.ShapeDtypeStruct(x.shape, jnp.bfloat16) for x in (queries, queries, keys, values)
        ),
        in_specs=[VMEM_SPEC] * 4,
        out_specs=(ANY_SPEC,) * 4,
        scratch_shapes=[
            pltpu.VMEM((2, ring // 2, 4, BLOCK, HEAD_WIDTH), jnp.bfloat16),
            pltpu.VMEM((4, BLOCK, HEAD_WIDTH), jnp.bfloat16),
        ]
        + link_semaphores(ring),
        compiler_params=pltpu.CompilerParams(
            collective_id=1, has_side_effects=True, vmem_limit_bytes=24 << 20
        ),
        name="scatter",
    )(o.reshape(tokens.shape), dq.reshape(tokens.shape), dk, dv)


def solution(mesh):
    placed = P(("dp", "context"), None)
    return jax.shard_map(
        local,
        mesh=mesh,
        in_specs=(placed, placed, placed, placed, P(), P()),
        out_specs=(placed,) * 4,
        check_vma=False,
    )
```

time: 859 us -> 112 us (0.13)
  waiting for transfers between devices: 259 us -> 0 us
  local copies, waits for them, and re-layouts: 186 us -> 7.96 us
  other arithmetic: 171 us -> 0 us
  Pallas kernels: 0 us -> 104 us
  loops' own time: 85 us -> 0 us
  blocking collectives: 60.7 us -> 0 us
  matrix products: 45.9 us -> 0 us
  starting transfers between devices: 42.9 us -> 0 us
    all_to_all x5 -> x0, waiting for transfers between devices: 214 us -> none  [the longest x1 54.3 us: local(): lax.all_to_all(owner_rows(queries, context_size, holder_split, query_port...]
    gather x129 -> x0, local copies, waits for them, and re-layouts: 152 us -> none  [the longest x32 57.5 us: backward(): key_tile = jnp.take(key_tiles, blocks, axis=0)]
    scatter-add x64 -> x0, other arithmetic: 148 us -> none  [the longest x32 74 us: backward(): key_sum.at[blocks]]
    pallas_call x0 -> x3, Pallas kernels: none -> 104 us  [the longest x1 44.2 us: local(): pl.pallas_call(functools.partial(scatter_kernel, ring), out_shape=tuple((...]
    another operation x25 -> x0, loops' own time: 85 us -> none  [the longest x8 28.6 us: one_group(): lax.fori_loop(0, head_count, backward, initial_grads)]
    all_to_all x1 -> x0, blocking collectives: 60.7 us -> none  [local(): lax.all_to_all(back_rows(output_rows), 'context', split_axis=0, concat_ax...]
    dot_general x192 -> x0, matrix products: 45.9 us -> none  [the longest x32 9.23 us: forward(): jnp.einsum('gqk,gkd->gqd', weights, value_tile, preferred_element_type=jn...]
    ppermute x2 -> x0, waiting for transfers between devices: 45.1 us -> none  [swapped(): return lax.ppermute(block, axis, route)]
  transfers between devices with their start and end apart: 7 -> 0, of which waited for: 7 -> 0; matrix products, arithmetic and copies ran while one was open for 2% -> 0% of each run, Pallas kernels for 0% -> 0%
where the time goes in v1:
time: 112 us; the launch traced here: 113 us
  Pallas kernels  104 us (93%)
  local copies, waits for them, and re-layouts  7.96 us (7%)
    pallas_call x1, Pallas kernels, local(): pl.pallas_call(functools.partial(scatter_kernel, ring), out_shape=tuple((...  44.2 us
    pallas_call x1, Pallas kernels, local(): pl.pallas_call(functools.partial(gather_kernel, ring), out_shape=(tokens,...  40.6 us
    pallas_call x1, Pallas kernels, attention(): pl.pallas_call(functools.partial(attention_kernel, ring, unroll), out_sha...  19.2 us
    unnamed x16, local copies, waits for them, and re-layouts  7.96 us

profile of v1, /device:TPU:1, one launch (start us, length us, event | category | flops | bytes accessed | tf_op | source)
XLA Modules:
  0.0 112.6 jit_solution(5191000393444334212)
XLA Ops:
  0.6 0.0 copy-start
  0.6 1.2 %copy-done = bf16[256,2048]{1,0:T(8,128)(2,1)S(1)} copy-done((bf16[256,2048]{1,0:T(8,128)(2,1)S(1)}, bf16[256,2048]{1,0:T(8,128)(2,1)}, u32[]{:S(2)}) %copy-start) | copy-done | bytes 1048600
  1.9 0.0 copy-start.1
  1.9 1.2 %copy-done.1 = bf16[256,2048]{1,0:T(8,128)(2,1)S(1)} copy-done((bf16[256,2048]{1,0:T(8,128)(2,1)S(1)}, bf16[256,2048]{1,0:T(8,128)(2,1)}, u32[]{:S(2)}) %copy-start.1) | copy-done | bytes 1048600
  3.1 0.0 copy-start.2
  3.1 0.8 copy-done.2
  3.9 0.0 copy-start.3
  3.9 0.8 copy-done.3
  4.8 0.0 copy-start.4
  4.8 40.6 %gather.1 = (bf16[4,256,512]{2,1,0:T(8,128)(2,1)S(1)}, bf16[4,256,512]{2,1,0:T(8,128)(2,1)S(1)}, bf16[32,128,128]{2,1,0:T(8,128)(2,1)S(1)}, bf16[32,128,128]{2,1,0:T(8,128)(2,1)S(1)}) custom-call(bf16[256,2048]{1,0:T(8,128)(2,1)S(1)} %copy-done, bf16[256,2048]{1,0:T(8,128)(2,1)S(1)} %copy-done.1, bf16[64,512]{1,0:T(8,128)(2,1)S(1)} %copy-done.2, ...), custom_call_target="tpu_custom_call" | custom-call | tf_op jit(solution)/shard_map/gather/pallas_call | solution.py:351
  45.3 0.0 copy-start.5
  45.4 0.0 copy-done.4
  45.4 0.6 copy-done.5
  46.0 19.2 %attention.1 = (bf16[8,128,512]{2,1,0:T(8,128)(2,1)S(1)}, bf16[8,128,512]{2,1,0:T(8,128)(2,1)S(1)}, bf16[32,128,128]{2,1,0:T(8,128)(2,1)S(1)}, bf16[32,128,128]{2,1,0:T(8,128)(2,1)S(1)}) custom-call(s32[16,4,128]{2,1,0:T(4,128)S(1)} %bitcast.9, s32[16]{0:T(128)S(1)} %copy-done.5, bf16[8,128,512]{2,1,0:T(8,128)(2,1)S(1)} %bitcast.5, ...), custom_call_target="tpu_custom_call" | custom-call | tf_op jit(solution)/shard_map/attention/pallas_call | solution.py:319
  65.2 44.2 %scatter.1 = (bf16[256,2048]{1,0:T(8,128)(2,1)S(1)}, bf16[256,2048]{1,0:T(8,128)(2,1)S(1)}, bf16[64,512]{1,0:T(8,128)(2,1)S(1)}, bf16[64,512]{1,0:T(8,128)(2,1)S(1)}) custom-call(bf16[4,256,512]{2,1,0:T(8,128)(2,1)S(1)} %bitcast.7, bf16[4,256,512]{2,1,0:T(8,128)(2,1)S(1)} %bitcast.8, bf16[32,128,128]{2,1,0:T(8,128)(2,1)S(1)} %get-tuple-element.18.dk, ...), custom_call_target="tpu_custom_call" | custom-call | tf_op jit(solution)/shard_map/scatter/pallas_call | solution.py:366
  109.4 1.0 copy.14
  110.4 1.0 copy.15
  111.3 0.6 copy.16
  112.0 0.6 copy.17
Async XLA Ops:
  0.6 1.2 %copy-start = (bf16[256,2048]{1,0:T(8,128)(2,1)S(1)}, bf16[256,2048]{1,0:T(8,128)(2,1)}, u32[]{:S(2)}) copy-start(bf16[256,2048]{1,0:T(8,128)(2,1)} %q.1) | copy-start | bytes 3145732
  1.9 1.2 %copy-start.1 = (bf16[256,2048]{1,0:T(8,128)(2,1)S(1)}, bf16[256,2048]{1,0:T(8,128)(2,1)}, u32[]{:S(2)}) copy-start(bf16[256,2048]{1,0:T(8,128)(2,1)} %g.1) | copy-start | bytes 3145732
  3.1 0.8 copy-start.2
  3.9 0.8 copy-start.3
  4.8 40.6 %copy-start.4 = (s32[16,128,4]{1,2,0:T(4,128)S(1)}, s32[16,128,4]{1,2,0:T(4,128)}, u32[]{:S(2)}) copy-start(s32[16,128,4]{1,2,0:T(4,128)} %param.10) | copy-start | bytes 98308
  45.3 0.7 copy-start.5

commit v2 on v1

v2 whole, which is shorter than its diff:
```python
import functools
import math

import jax
import jax.numpy as jnp
from jax import lax
from jax.experimental import pallas as pl
from jax.experimental.pallas import tpu as pltpu
from jax.sharding import PartitionSpec as P

QUERY_HEADS = 16
KEY_VALUE_HEADS = 4
HEAD_WIDTH = 128
BLOCK = 128
GROUP_WIDTH = 4 * HEAD_WIDTH
MESH = pl.DeviceIdType.MESH
VMEM_SPEC = pl.BlockSpec(memory_space=pltpu.VMEM)
ANY_SPEC = pl.BlockSpec(memory_space=pl.ANY)
HBM_SPEC = pl.BlockSpec(memory_space=pltpu.HBM)
SCALE = 1.0 / math.sqrt(HEAD_WIDTH)
SCALE_LOG2E = SCALE / math.log(2.0)
ROUTES = ((0, 0), (0, 1), (1, 0), (1, 1))


class Place:
    def __init__(self, ring):
        dp = lax.axis_index("dp")
        context = lax.axis_index("context")
        self.ring = ring
        self.dp = dp
        self.member = dp % 2
        self.core = context % 2
        self.z = context // 2
        self.head = self.member * 2 + self.core

    def partner(self, route, step=0):
        flip_member, flip_core = route
        member = 1 - self.member if flip_member else self.member
        core = 1 - self.core if flip_core else self.core
        z = (self.z + step + self.ring) % self.ring
        return member, core, member * 2 + core, (self.dp - self.member + member, z * 2 + core)

    def greet(self):
        barrier = pltpu.get_barrier_semaphore()
        others = [
            self.partner(route, step)[3] for step in (1, -1, 0) for route in ROUTES if step or any(route)
        ]
        for other in others:
            pl.semaphore_signal(barrier, inc=1, device_id=other, device_id_type=MESH)
        return barrier, len(others)


def columns(index, width):
    return pl.ds(pl.multiple_of(index * width, width), width)


def remote(source, landing, send_sem, recv_sem, device):
    return pltpu.make_async_remote_copy(
        src_ref=source,
        dst_ref=landing,
        send_sem=send_sem,
        recv_sem=recv_sem,
        device_id=device,
        device_id_type=MESH,
    )


SIGNS = (1, -1)
PIECES = [(t, i) for i in (2, 3, 1, 0) for t in range(2)]


def gather_kernel(
    ring, q, g, k, v, qg, gg, kf, vf, kt, vt, own_sem, send_x, recv_x, send_z, recv_z
):
    place = Place(ring)
    barrier, expected = place.greet()
    pl.semaphore_wait(barrier, expected)
    half = k.shape[0]
    far = ring // 2

    def rows(buffer, route, z):
        member, core, _, _ = place.partner(route)
        return buffer.at[member * ring + z, columns(core, half), :]

    def chunk_z(way, chunk):
        return (place.z - SIGNS[way] * chunk + ring) % ring

    first, near = [], []
    for t, i in PIECES:
        piece = (k, v)[t].at[:, columns(place.partner(ROUTES[i])[2], HEAD_WIDTH)]
        landing = rows((kf, vf)[t], ROUTES[0], place.z)
        for way in range(2):
            first.append(
                remote(
                    piece,
                    landing,
                    send_z.at[way, 0, t * 4 + i],
                    recv_z.at[way, 0, t * 4 + i],
                    place.partner(ROUTES[i], SIGNS[way])[3],
                )
            )
            first[-1].start()
    for t, i in PIECES:
        piece = (k, v)[t].at[:, columns(place.partner(ROUTES[i])[2], HEAD_WIDTH)]
        landing = rows((kf, vf)[t], ROUTES[0], place.z)
        if i == 0:
            copy = pltpu.make_async_copy(piece, landing, own_sem.at[t])
        else:
            copy = remote(
                piece,
                landing,
                send_x.at[t, i - 1],
                recv_x.at[t, i - 1],
                place.partner(ROUTES[i])[3],
            )
        near.append((i, copy))
        copy.start()
    large = []
    for t, (source, target) in enumerate(((q, qg), (g, gg))):
        for i in (2, 3, 1, 0):
            _, _, head, device = place.partner(ROUTES[i])
            piece = source.at[:, columns(head, GROUP_WIDTH)]
            landing = target.at[place.head]
            if i == 0:
                copy = pltpu.make_async_copy(piece, landing, own_sem.at[2 + t])
            else:
                copy = remote(
                    piece, landing, send_x.at[2 + t, i - 1], recv_x.at[2 + t, i - 1], device
                )
            large.append(copy)
            copy.start()

    def hop(way, chunk, slot, t, i):
        piece = rows((kf, vf)[t], ROUTES[i], chunk_z(way, chunk))
        return remote(
            piece,
            piece,
            send_z.at[way, slot, t * 4 + i],
            recv_z.at[way, slot, t * 4 + i],
            place.partner(ROUTES[0], SIGNS[way])[3],
        )

    def turn(z):
        for member in range(2):
            block = member * ring + z
            kt[block] = kf[block].T
            vt[block] = vf[block].T

    def forward(step, carry):
        for t, i in reversed(PIECES):
            for way in range(2):
                hop(way, step, step - 1, t, i).wait_recv()
                hop(way, step, step, t, i).start()
        for way in range(2):
            turn(chunk_z(way, step))
        return carry

    lax.fori_loop(1, far - 1, forward, 0)
    for t, i in reversed(PIECES):
        for way in range(2):
            hop(way, far - 1, far - 2, t, i).wait_recv()
            if i % 2 == way:
                hop(way, far - 1, far - 1, t, i).start()
    for way in range(2):
        turn(chunk_z(way, far - 1))
    for i, copy in near:
        copy.wait() if i == 0 else copy.wait_recv()
    turn(place.z)
    for t, i in reversed(PIECES):
        hop(i % 2, far, far - 1, t, i).wait_recv()
    turn(chunk_z(0, far))

    def drain(step, carry):
        for t, i in PIECES:
            for way in range(2):
                hop(way, step, step, t, i).wait_send()
        return carry

    for copy in first:
        copy.wait_send()
    lax.fori_loop(1, far - 1, drain, 0)
    for t, i in PIECES:
        hop(i % 2, far - 1, far - 1, t, i).wait_send()
    for i, copy in near:
        if i > 0:
            copy.wait_send()
    for copy in large:
        copy.wait()


def scatter_kernel(
    ring, o, dq, dk, dv, att, dqo, dko, dvo, first, own, landed, own_sem, send_x, recv_x, send_z, recv_z
):
    place = Place(ring)
    barrier, expected = place.greet()
    half = dko.shape[0]
    far = ring // 2

    def partial(way, distance, t, i):
        member, core, _, _ = place.partner(ROUTES[i])
        z = (place.z + SIGNS[way] * distance + ring) % ring
        return (dk, dv)[t][member * ring + z, columns(core, half), :]

    def longer(way, i):
        return i % 2 == way

    for t, i in PIECES:
        for way in range(2):
            distance = far if longer(way, i) else far - 1
            first[way, t * 4 + i] = partial(way, distance, t, i).astype(jnp.bfloat16)
    pl.semaphore_wait(barrier, expected)

    def hop(source, way, slot, t, i, last=False):
        return remote(
            source,
            landed.at[way, slot, t * 4 + i],
            send_z.at[way, slot, t * 4 + i],
            recv_z.at[way, slot, t * 4 + i],
            place.partner(ROUTES[i if last else 0], SIGNS[way])[3],
        )

    def pass_on(way, distance, t, i, last=False):
        slot = landed.at[way, distance, t * 4 + i]
        hop(slot, way, distance, t, i).wait_recv()
        slot[...] = (slot[...].astype(jnp.float32) + partial(way, distance, t, i)).astype(
            jnp.bfloat16
        )
        hop(slot, way, distance - 1, t, i, last).start()

    for t, i in PIECES:
        for way in range(2):
            distance = far if longer(way, i) else far - 1
            hop(first.at[way, t * 4 + i], way, distance - 1, t, i).start()
    copies = []
    for t, i in PIECES:
        piece = t * 4 + i
        own[0, piece] = partial(0, 0, t, i).astype(jnp.bfloat16)
        if i > 0:
            copies.append(
                remote(
                    own.at[0, piece],
                    own.at[1, piece],
                    send_x.at[2 + t, i - 1],
                    recv_x.at[2 + t, i - 1],
                    place.partner(ROUTES[i])[3],
                )
            )
            copies[-1].start()
    for t, (source, target) in enumerate(((o, att), (dq, dqo))):
        for i in (2, 3, 1, 0):
            _, _, head, device = place.partner(ROUTES[i])
            landing = target.at[:, columns(place.head, GROUP_WIDTH)]
            if i == 0:
                copy = pltpu.make_async_copy(source.at[head], landing, own_sem.at[t])
            else:
                copy = remote(
                    source.at[head], landing, send_x.at[t, i - 1], recv_x.at[t, i - 1], device
                )
            copies.append(copy)
            copy.start()
    for t, i in PIECES:
        pass_on(i % 2, far - 1, t, i)

    def steps(n, carry):
        for t, i in PIECES:
            for way in range(2):
                pass_on(way, far - 2 - n, t, i)
        return carry

    lax.fori_loop(0, far - 3, steps, 0)
    for t, i in PIECES:
        for way in range(2):
            pass_on(way, 1, t, i, True)
    for copy in copies[:6]:
        copy.wait_recv()
    for t, i in reversed(PIECES):
        piece = t * 4 + i
        for way in range(2):
            hop(landed.at[way, 0, piece], way, 0, t, i, True).wait_recv()
        total = landed[0, 0, piece].astype(jnp.float32) + landed[1, 0, piece].astype(jnp.float32)
        total = total + own[1 if i > 0 else 0, piece].astype(jnp.float32)
        if t == 0:
            total = total * SCALE
        (dko, dvo)[t][:, columns(place.partner(ROUTES[i])[2], HEAD_WIDTH)] = total.astype(
            jnp.bfloat16
        )

    def drain(step, carry):
        for t, i in PIECES:
            for way in range(2):
                hop(landed.at[way, step, t * 4 + i], way, step, t, i).wait_send()
        return carry

    lax.fori_loop(1, far - 1, drain, 0)
    for t, i in PIECES:
        for way in range(2):
            hop(landed.at[way, 0, t * 4 + i], way, 0, t, i, True).wait_send()
        hop(landed.at[i % 2, far - 1, t * 4 + i], i % 2, far - 1, t, i).wait_send()
    for n, copy in enumerate(copies):
        if n < 6:
            copy.wait_send()
        else:
            copy.wait()


def output_kernel(*refs):
    sources, targets, sems = refs[:4], refs[4:8], refs[8]
    copies = [
        pltpu.make_async_copy(source, target, sems.at[n])
        for n, (source, target) in enumerate(zip(sources, targets))
    ]
    for copy in copies:
        copy.start()
    for copy in copies:
        copy.wait()


def attend(count, unroll, z_blocks, head, start, q, g, k, v, kt, vt, o, dq, dka, dva, picked):
    lanes = columns(head, HEAD_WIDTH)
    nt = (((1,), (1,)), ((), ()))
    results = []
    for u in range(unroll):
        qi = start + u
        block = qi // 4 * (z_blocks * 4) + qi % 4
        chosen = [picked(head, j, block) for j in range(count)]
        query = q[qi, :, lanes]
        grad = g[qi, :, lanes]
        scores = lax.dot_general(
            jnp.concatenate([k[b] for b in chosen], 0), query, nt, preferred_element_type=jnp.float32
        )
        dweights = lax.dot_general(
            jnp.concatenate([v[b] for b in chosen], 0), grad, nt, preferred_element_type=jnp.float32
        )
        peak = jnp.max(scores, axis=0, keepdims=True)
        powers = jnp.exp2((scores - peak) * SCALE_LOG2E)
        weights = powers * (1.0 / jnp.sum(powers, axis=0, keepdims=True))
        delta = jnp.sum(weights * dweights, axis=0, keepdims=True)
        dscores = (weights * (dweights - delta)).astype(jnp.bfloat16)
        weights = weights.astype(jnp.bfloat16)
        out = jnp.dot(
            jnp.concatenate([vt[b] for b in chosen], 1), weights, preferred_element_type=jnp.float32
        )
        o[qi, :, lanes] = out.T.astype(jnp.bfloat16)
        dquery = jnp.dot(
            jnp.concatenate([kt[b] for b in chosen], 1), dscores, preferred_element_type=jnp.float32
        )
        dq[qi, :, lanes] = (dquery.T * SCALE).astype(jnp.bfloat16)
        dkey = jnp.dot(dscores, query, preferred_element_type=jnp.float32)
        dvalue = jnp.dot(weights, grad, preferred_element_type=jnp.float32)
        results.append((chosen, dkey, dvalue))
    for chosen, dkey, dvalue in results:
        for j, b in enumerate(chosen):
            rows = slice(j * BLOCK, (j + 1) * BLOCK)
            dka[b] += dkey[rows]
            dva[b] += dvalue[rows]


def attention_kernel(ring, unroll, lists, counts, q, g, k, v, kt, vt, o, dq, dk, dv, own_lists, sem):
    place = Place(ring)
    copy = pltpu.make_async_copy(lists.at[pl.ds(place.head * 4, 4)], own_lists, sem)
    copy.start()

    @pl.loop(0, k.shape[0])
    def _(b):
        dk[b] = jnp.zeros((BLOCK, HEAD_WIDTH), jnp.float32)
        dv[b] = jnp.zeros((BLOCK, HEAD_WIDTH), jnp.float32)

    copy.wait()

    def picked(head, j, block):
        return own_lists[head, j, place.z * 4 + block]

    @pl.loop(0, 4)
    def _(head):
        used = counts[place.head * 4 + head]
        for count in range(1, 5):

            @pl.when(used == count)
            def _():
                @pl.loop(0, 8, step=unroll)
                def _(start):
                    attend(
                        count, unroll, ring, head, start, q, g, k, v, kt, vt, o, dq, dk, dv, picked
                    )


def attention(ring, lists, counts, qg, gg, kf, vf, kt, vt, unroll=2):
    tokens = jax.ShapeDtypeStruct((8, BLOCK, GROUP_WIDTH), jnp.bfloat16)
    rows = jax.ShapeDtypeStruct(kf.shape, jnp.float32)
    return pl.pallas_call(
        functools.partial(attention_kernel, ring, unroll),
        out_shape=(tokens, tokens, rows, rows),
        in_specs=[ANY_SPEC, pl.BlockSpec(memory_space=pltpu.SMEM)] + [VMEM_SPEC] * 6,
        out_specs=(VMEM_SPEC,) * 4,
        scratch_shapes=[
            pltpu.SMEM((4, 4, lists.shape[2]), jnp.int32),
            pltpu.SemaphoreType.DMA,
        ],
        compiler_params=pltpu.CompilerParams(vmem_limit_bytes=32 << 20),
        name="attention",
    )(lists, counts, qg, gg, kf, vf, kt, vt)


def link_semaphores(ring):
    return [
        pltpu.SemaphoreType.DMA((4,)),
        pltpu.SemaphoreType.DMA((4, 3)),
        pltpu.SemaphoreType.DMA((4, 3)),
        pltpu.SemaphoreType.DMA((2, ring // 2, 8)),
        pltpu.SemaphoreType.DMA((2, ring // 2, 8)),
    ]


def local(queries, keys, values, grad_out, layout, counts):
    ring = lax.axis_size("context") // 2
    half = keys.shape[0]
    tokens = jax.ShapeDtypeStruct((4, queries.shape[0], GROUP_WIDTH), jnp.bfloat16)
    rows = jax.ShapeDtypeStruct((2 * ring, BLOCK, HEAD_WIDTH), jnp.bfloat16)
    outs = tuple(
        jax.ShapeDtypeStruct(x.shape, jnp.bfloat16) for x in (queries, queries, keys, values)
    )
    qg, gg, kf, vf, kt, vt = pl.pallas_call(
        functools.partial(gather_kernel, ring),
        out_shape=(tokens, tokens, rows, rows, rows, rows),
        in_specs=[HBM_SPEC] * 4,
        out_specs=(VMEM_SPEC,) * 6,
        scratch_shapes=link_semaphores(ring),
        compiler_params=pltpu.CompilerParams(
            collective_id=0, has_side_effects=True, vmem_limit_bytes=47 << 20
        ),
        name="gather",
    )(queries, grad_out, keys, values)
    shape = (8, BLOCK, GROUP_WIDTH)
    o, dq, dk, dv = attention(
        ring,
        layout.transpose(0, 2, 1),
        counts,
        qg.reshape(shape),
        gg.reshape(shape),
        kf,
        vf,
        kt,
        vt,
    )
    results = pl.pallas_call(
        functools.partial(scatter_kernel, ring),
        out_shape=outs,
        in_specs=[VMEM_SPEC] * 4,
        out_specs=(VMEM_SPEC,) * 4,
        scratch_shapes=[
            pltpu.VMEM((2, 8, half, HEAD_WIDTH), jnp.bfloat16),
            pltpu.VMEM((2, 8, half, HEAD_WIDTH), jnp.bfloat16),
            pltpu.VMEM((2, ring // 2, 8, half, HEAD_WIDTH), jnp.bfloat16),
        ]
        + link_semaphores(ring),
        compiler_params=pltpu.CompilerParams(
            collective_id=1, has_side_effects=True, vmem_limit_bytes=24 << 20
        ),
        name="scatter",
    )(o.reshape(tokens.shape), dq.reshape(tokens.shape), dk, dv)
    return pl.pallas_call(
        output_kernel,
        out_shape=outs,
        in_specs=[ANY_SPEC] * 4,
        out_specs=(HBM_SPEC,) * 4,
        scratch_shapes=[pltpu.SemaphoreType.DMA((4,))],
        compiler_params=pltpu.CompilerParams(vmem_limit_bytes=1 << 20),
        name="output",
    )(*results)


def solution(mesh):
    placed = P(("dp", "context"), None)
    return jax.shard_map(
        local,
        mesh=mesh,
        in_specs=(placed, placed, placed, placed, P(), P()),
        out_specs=(placed,) * 4,
        check_vma=False,
    )
```

time: 112 us -> 100 us (0.89)
  Pallas kernels: 104 us -> 97.1 us
  local copies, waits for them, and re-layouts: 7.96 us -> 1.69 us
    pallas_call x1 -> x2, Pallas kernels: 44.2 us -> 35.8 us  [the longest x1 34.4 us: local(): pl.pallas_call(functools.partial(scatter_kernel, ring), out_shape=outs, i...]
    unnamed x16 -> x8, local copies, waits for them, and re-layouts: 7.96 us -> 1.69 us
    pallas_call x1, Pallas kernels: 40.6 us -> 41.7 us  [local(): pl.pallas_call(functools.partial(gather_kernel, ring), out_shape=(tokens,...]
where the time goes in v2:
time: 100 us; the launch traced here: 99.5 us
  Pallas kernels  97.1 us (97%)
  local copies, waits for them, and re-layouts  1.69 us (2%)
    pallas_call x1, Pallas kernels, local(): pl.pallas_call(functools.partial(gather_kernel, ring), out_shape=(tokens,...  41.7 us
    pallas_call x1, Pallas kernels, local(): pl.pallas_call(functools.partial(scatter_kernel, ring), out_shape=outs, i...  34.4 us
    pallas_call x1, Pallas kernels, attention(): pl.pallas_call(functools.partial(attention_kernel, ring, unroll), out_sha...  19.6 us

profile of v2, /device:TPU:1, one launch (start us, length us, event | category | flops | bytes accessed | tf_op | source)
XLA Modules:
  0.0 99.5 jit_solution(177542657452080894)
XLA Ops:
  0.6 0.0 copy-start.3
  0.6 0.0 copy-start
  0.7 0.8 copy-done
  1.5 0.0 copy-start.1
  1.5 0.8 copy-done.1
  2.3 0.0 copy-start.2
  2.3 41.7 %gather.1 = (bf16[4,256,512]{2,1,0:T(8,128)(2,1)S(1)}, bf16[4,256,512]{2,1,0:T(8,128)(2,1)S(1)}, bf16[32,128,128]{2,1,0:T(8,128)(2,1)S(1)}, bf16[32,128,128]{2,1...) custom-call(bf16[256,2048]{1,0:T(8,128)(2,1)} %q.1, bf16[256,2048]{1,0:T(8,128)(2,1)} %g.1, ...), custom_call_target="tpu_custom_call" | custom-call | tf_op jit(solution)/shard_map/gather/pallas_call | solution.py:422
  44.1 0.0 copy-done.3
  44.1 0.0 copy-done.2
  44.1 19.6 %attention.1 = (bf16[8,128,512]{2,1,0:T(8,128)(2,1)S(1)}, bf16[8,128,512]{2,1,0:T(8,128)(2,1)S(1)}, f32[32,128,128]{2,1,0:T(8,128)S(1)}, f32[32,128,128]{2,1,0:T(8,128)S(1)}) custom-call(s32[16,4,128]{2,1,0:T(4,128)S(1)} %bitcast.9, s32[16]{0:T(128)S(1)} %copy-done.3, bf16[8,128,512]{2,1,0:T(8,128)(2,1)S(1)} %bitcast.5, bf16[8,128,512]{2,1,0:T(8,128)(2,1)S(1)} %bitcast.6, ...), custom_call_target="tpu_custom_call" | custom-call | tf_op jit(solution)/shard_map/attention/pallas_call | solution.py:390
  63.7 34.4 %scatter.1 = (bf16[256,2048]{1,0:T(8,128)(2,1)S(1)}, bf16[256,2048]{1,0:T(8,128)(2,1)S(1)}, bf16[64,512]{1,0:T(8,128)(2,1)S(1)}, bf16[64,512]{1,0:T(8,128)(2,1)S(1)}) custom-call(bf16[4,256,512]{2,1,0:T(8,128)(2,1)S(1)} %bitcast.7, bf16[4,256,512]{2,1,0:T(8,128)(2,1)S(1)} %bitcast.8, f32[32,128,128]{2,1,0:T(8,128)S(1)} %get-tuple-element.26.dk, ...), custom_call_target="tpu_custom_call" | custom-call | tf_op jit(solution)/shard_map/scatter/pallas_call | solution.py:445
  98.1 1.4 %output.1 = (bf16[256,2048]{1,0:T(8,128)(2,1)}, bf16[256,2048]{1,0:T(8,128)(2,1)}, bf16[64,512]{1,0:T(8,128)(2,1)}, bf16[64,512]{1,0:T(8,128)(2,1)}) custom-call(bf16[256,2048]{1,0:T(8,128)(2,1)S(1)} %get-tuple-element.28.refs_0_, bf16[256,2048]{1,0:T(8,128)(2,1)S(1)} %get-tuple-element.29.refs_1_, bf16[64,512]{1,0:T(8,128)(2,1)S(1)} %get-tuple-element.30.refs_2_, ...), custom_call_target="tpu_custom_call" | custom-call | tf_op jit(solution)/shard_map/output/pallas_call | solution.py:461
Async XLA Ops:
  0.6 43.4 %copy-start.3 = (s32[16]{0:T(128)S(1)}, s32[16]{0:T(128)}, u32[]{:S(2)}) copy-start(s32[16]{0:T(128)} %counts.1) | copy-start | bytes 196
  0.6 0.8 copy-start
  1.5 0.8 copy-start.1
  2.3 41.8 %copy-start.2 = (s32[16,128,4]{1,2,0:T(4,128)S(1)}, s32[16,128,4]{1,2,0:T(4,128)}, u32[]{:S(2)}) copy-start(s32[16,128,4]{1,2,0:T(4,128)} %param.10) | copy-start | bytes 98308

commit v3 on v2

--- a/solution.py
+++ b/solution.py
@@ -189,10 +189,35 @@
 
 
 def scatter_kernel(
-    ring, o, dq, dk, dv, att, dqo, dko, dvo, first, own, landed, own_sem, send_x, recv_x, send_z, recv_z
+    ring,
+    lists,
+    wt,
+    ds,
+    kt,
+    vt,
+    dk,
+    dv,
+    att,
+    dqo,
+    dko,
+    dvo,
+    o,
+    dq,
+    first,
+    own,
+    landed,
+    own_lists,
+    list_sem,
+    own_sem,
+    send_x,
+    recv_x,
+    send_z,
+    recv_z,
 ):
     place = Place(ring)
     barrier, expected = place.greet()
+    list_copy = pltpu.make_async_copy(lists.at[pl.ds(place.head * 4, 4)], own_lists, list_sem)
+    list_copy.start()
     half = dko.shape[0]
     far = ring // 2
 
@@ -246,28 +271,56 @@
                 )
             )
             copies[-1].start()
-    for t, (source, target) in enumerate(((o, att), (dq, dqo))):
-        for i in (2, 3, 1, 0):
-            _, _, head, device = place.partner(ROUTES[i])
+    def finish(i):
+        _, _, slot, device = place.partner(ROUTES[i])
+        for block in range(2):
+            qi = slot * 2 + block
+            at = place.z * 4 + qi // 4 * (ring * 4) + qi % 4
+            rows = slice(block * BLOCK, (block + 1) * BLOCK)
+            for head in range(4):
+                lanes = slice(head * HEAD_WIDTH, (head + 1) * HEAD_WIDTH)
+                chosen = [own_lists[head, j, at] for j in range(4)]
+                out = jnp.dot(
+                    jnp.concatenate([vt[b] for b in chosen], 1),
+                    wt[qi * 4 + head],
+                    preferred_element_type=jnp.float32,
+                )
+                o[slot, rows, lanes] = out.T.astype(jnp.bfloat16)
+                out = jnp.dot(
+                    jnp.concatenate([kt[b] for b in chosen], 1),
+                    ds[qi * 4 + head],
+                    preferred_element_type=jnp.float32,
+                )
+                dq[slot, rows, lanes] = (out.T * SCALE).astype(jnp.bfloat16)
+        for t, (source, target) in enumerate(((o, att), (dq, dqo))):
             landing = target.at[:, columns(place.head, GROUP_WIDTH)]
             if i == 0:
-                copy = pltpu.make_async_copy(source.at[head], landing, own_sem.at[t])
+                copy = pltpu.make_async_copy(source.at[slot], landing, own_sem.at[t])
             else:
                 copy = remote(
-                    source.at[head], landing, send_x.at[t, i - 1], recv_x.at[t, i - 1], device
+                    source.at[slot], landing, send_x.at[t, i - 1], recv_x.at[t, i - 1], device
                 )
             copies.append(copy)
             copy.start()
+
+    list_copy.wait()
+    finish(2)
     for t, i in PIECES:
         pass_on(i % 2, far - 1, t, i)
+    finish(3)
+    for distance in (far - 2, far - 3):
+        for t, i in PIECES:
+            for way in range(2):
+                pass_on(way, distance, t, i)
+        finish(far - 1 - distance if distance == far - 2 else 0)
 
     def steps(n, carry):
         for t, i in PIECES:
             for way in range(2):
-                pass_on(way, far - 2 - n, t, i)
+                pass_on(way, far - 4 - n, t, i)
         return carry
 
-    lax.fori_loop(0, far - 3, steps, 0)
+    lax.fori_loop(0, far - 5, steps, 0)
     for t, i in PIECES:
         for way in range(2):
             pass_on(way, 1, t, i, True)
@@ -315,7 +368,7 @@
         copy.wait()
 
 
-def attend(count, unroll, z_blocks, head, start, q, g, k, v, kt, vt, o, dq, dka, dva, picked):
+def attend(count, unroll, z_blocks, head, start, q, g, k, v, wt, ds, dk, dv, picked):
     lanes = columns(head, HEAD_WIDTH)
     nt = (((1,), (1,)), ((), ()))
     results = []
@@ -337,25 +390,24 @@
         delta = jnp.sum(weights * dweights, axis=0, keepdims=True)
         dscores = (weights * (dweights - delta)).astype(jnp.bfloat16)
         weights = weights.astype(jnp.bfloat16)
-        out = jnp.dot(
-            jnp.concatenate([vt[b] for b in chosen], 1), weights, preferred_element_type=jnp.float32
-        )
-        o[qi, :, lanes] = out.T.astype(jnp.bfloat16)
-        dquery = jnp.dot(
-            jnp.concatenate([kt[b] for b in chosen], 1), dscores, preferred_element_type=jnp.float32
-        )
-        dq[qi, :, lanes] = (dquery.T * SCALE).astype(jnp.bfloat16)
+        item = qi * 4 + head
+        wt[item, : count * BLOCK] = weights
+        ds[item, : count * BLOCK] = dscores
+        if count < 4:
+            rest = jnp.zeros(((4 - count) * BLOCK, BLOCK), jnp.bfloat16)
+            wt[item, count * BLOCK :] = rest
+            ds[item, count * BLOCK :] = rest
         dkey = jnp.dot(dscores, query, preferred_element_type=jnp.float32)
         dvalue = jnp.dot(weights, grad, preferred_element_type=jnp.float32)
         results.append((chosen, dkey, dvalue))
     for chosen, dkey, dvalue in results:
         for j, b in enumerate(chosen):
             rows = slice(j * BLOCK, (j + 1) * BLOCK)
-            dka[b] += dkey[rows]
-            dva[b] += dvalue[rows]
-
-
-def attention_kernel(ring, unroll, lists, counts, q, g, k, v, kt, vt, o, dq, dk, dv, own_lists, sem):
+            dk[b] += dkey[rows]
+            dv[b] += dvalue[rows]
+
+
+def attention_kernel(ring, unroll, lists, counts, q, g, k, v, wt, ds, dk, dv, own_lists, sem):
     place = Place(ring)
     copy = pltpu.make_async_copy(lists.at[pl.ds(place.head * 4, 4)], own_lists, sem)
     copy.start()
@@ -379,18 +431,16 @@
             def _():
                 @pl.loop(0, 8, step=unroll)
                 def _(start):
-                    attend(
-                        count, unroll, ring, head, start, q, g, k, v, kt, vt, o, dq, dk, dv, picked
-                    )
-
-
-def attention(ring, lists, counts, qg, gg, kf, vf, kt, vt, unroll=2):
-    tokens = jax.ShapeDtypeStruct((8, BLOCK, GROUP_WIDTH), jnp.bfloat16)
+                    attend(count, unroll, ring, head, start, q, g, k, v, wt, ds, dk, dv, picked)
+
+
+def attention(ring, lists, counts, qg, gg, kf, vf, unroll=2):
+    items = jax.ShapeDtypeStruct((32, 4 * BLOCK, BLOCK), jnp.bfloat16)
     rows = jax.ShapeDtypeStruct(kf.shape, jnp.float32)
     return pl.pallas_call(
         functools.partial(attention_kernel, ring, unroll),
-        out_shape=(tokens, tokens, rows, rows),
-        in_specs=[ANY_SPEC, pl.BlockSpec(memory_space=pltpu.SMEM)] + [VMEM_SPEC] * 6,
+        out_shape=(items, items, rows, rows),
+        in_specs=[ANY_SPEC, pl.BlockSpec(memory_space=pltpu.SMEM)] + [VMEM_SPEC] * 4,
         out_specs=(VMEM_SPEC,) * 4,
         scratch_shapes=[
             pltpu.SMEM((4, 4, lists.shape[2]), jnp.int32),
@@ -398,7 +448,7 @@
         ],
         compiler_params=pltpu.CompilerParams(vmem_limit_bytes=32 << 20),
         name="attention",
-    )(lists, counts, qg, gg, kf, vf, kt, vt)
+    )(lists, counts, qg, gg, kf, vf)
 
 
 def link_semaphores(ring):
@@ -431,33 +481,28 @@
         name="gather",
     )(queries, grad_out, keys, values)
     shape = (8, BLOCK, GROUP_WIDTH)
-    o, dq, dk, dv = attention(
-        ring,
-        layout.transpose(0, 2, 1),
-        counts,
-        qg.reshape(shape),
-        gg.reshape(shape),
-        kf,
-        vf,
-        kt,
-        vt,
-    )
+    lists = layout.transpose(0, 2, 1)
+    wt, ds, dk, dv = attention(ring, lists, counts, qg.reshape(shape), gg.reshape(shape), kf, vf)
     results = pl.pallas_call(
         functools.partial(scatter_kernel, ring),
         out_shape=outs,
-        in_specs=[VMEM_SPEC] * 4,
+        in_specs=[ANY_SPEC] + [VMEM_SPEC] * 6,
         out_specs=(VMEM_SPEC,) * 4,
         scratch_shapes=[
+            pltpu.VMEM(tokens.shape, jnp.bfloat16),
+            pltpu.VMEM(tokens.shape, jnp.bfloat16),
             pltpu.VMEM((2, 8, half, HEAD_WIDTH), jnp.bfloat16),
             pltpu.VMEM((2, 8, half, HEAD_WIDTH), jnp.bfloat16),
             pltpu.VMEM((2, ring // 2, 8, half, HEAD_WIDTH), jnp.bfloat16),
+            pltpu.SMEM((4, 4, lists.shape[2]), jnp.int32),
+            pltpu.SemaphoreType.DMA,
         ]
         + link_semaphores(ring),
         compiler_params=pltpu.CompilerParams(
             collective_id=1, has_side_effects=True, vmem_limit_bytes=24 << 20
         ),
         name="scatter",
-    )(o.reshape(tokens.shape), dq.reshape(tokens.shape), dk, dv)
+    )(lists, wt, ds, kt, vt, dk, dv)
     return pl.pallas_call(
         output_kernel,
         out_shape=outs,

time: 100 us -> 100 us (level)
  local copies, waits for them, and re-layouts: 1.69 us -> 3.08 us
  Pallas kernels: 97.1 us -> 96 us
    pallas_call x1, Pallas kernels: 19.6 us -> 13.1 us  [attention(): pl.pallas_call(functools.partial(attention_kernel, ring, unroll), out_sha...]
    pallas_call x1, Pallas kernels: 34.4 us -> 39.9 us  [local(): pl.pallas_call(functools.partial(scatter_kernel, ring), out_shape=outs, i...]
    unnamed x8, local copies, waits for them, and re-layouts: 1.69 us -> 3.08 us
where the time goes in v3:
time: 100 us; the launch traced here: 99.7 us
  Pallas kernels  96 us (96%)
  local copies, waits for them, and re-layouts  3.08 us (3%)
    pallas_call x1, Pallas kernels, local(): pl.pallas_call(functools.partial(gather_kernel, ring), out_shape=(tokens,...  41.6 us
    pallas_call x1, Pallas kernels, local(): pl.pallas_call(functools.partial(scatter_kernel, ring), out_shape=outs, i...  39.9 us
    pallas_call x1, Pallas kernels, attention(): pl.pallas_call(functools.partial(attention_kernel, ring, unroll), out_sha...  13.1 us
    unnamed x8, local copies, waits for them, and re-layouts  3.08 us

profile of v3, /device:TPU:1, one launch (start us, length us, event | category | flops | bytes accessed | tf_op | source)
XLA Modules:
  0.0 99.7 jit_solution(3186040307402274904)
XLA Ops:
  0.6 0.0 copy-start.1
  0.6 0.8 copy-done.1
  1.5 0.0 copy-start.2
  1.5 0.8 copy-done.2
  2.3 41.6 %gather.1 = (bf16[4,256,512]{2,1,0:T(8,128)(2,1)S(1)}, bf16[4,256,512]{2,1,0:T(8,128)(2,1)S(1)}, bf16[32,128,128]{2,1,0:T(8,128)(2,1)S(1)}, bf16[32,128,128]{2,1...) custom-call(bf16[256,2048]{1,0:T(8,128)(2,1)} %q.1, bf16[256,2048]{1,0:T(8,128)(2,1)} %g.1, ...), custom_call_target="tpu_custom_call" | custom-call | tf_op jit(solution)/shard_map/gather/pallas_call | solution.py:472
  43.9 0.0 copy-start
  43.9 0.7 copy-done
  44.7 0.0 copy-start.3
  44.7 0.7 copy-done.3
  45.3 13.1 %attention.1 = (bf16[32,512,128]{2,1,0:T(8,128)(2,1)S(1)}, bf16[32,512,128]{2,1,0:T(8,128)(2,1)S(1)}, f32[32,128,128]{2,1,0:T(8,128)S(1)}, f32[32,128,128]{2,1,0:T(8,128)S(1)}) custom-call(s32[16,4,128]{2,1,0:T(4,128)S(1)} %bitcast.5, s32[16]{0:T(128)S(1)} %copy-done.3, bf16[8,128,512]{2,1,0:T(8,128)(2,1)S(1)} %bitcast.3, bf16[8,128,512]{2,1,0:T(8,128)(2,1)S(1)} %bitcast.4, ...), custom_call_target="tpu_custom_call" | custom-call | tf_op jit(solution)/shard_map/attention/pallas_call | solution.py:440
  58.5 39.9 %scatter.1 = (bf16[256,2048]{1,0:T(8,128)(2,1)S(1)}, bf16[256,2048]{1,0:T(8,128)(2,1)S(1)}, bf16[64,512]{1,0:T(8,128)(2,1)S(1)}, bf16[64,512]{1,0:T(8,128)(2,1)S(1)}) custom-call(s32[16,4,128]{2,1,0:T(4,128)S(1)} %bitcast.6, bf16[32,512,128]{2,1,0:T(8,128)(2,1)S(1)} %get-tuple-element.22.wt, bf16[32,512,128]{2,1,0:T(8,128)(2,1)S(1)} %get-tuple-element.23.ds, ...), custom_call_target="tpu_custom_call" | custom-call | tf_op jit(solution)/shard_map/scatter/pallas_call | solution.py:486
  98.4 1.4 %output.1 = (bf16[256,2048]{1,0:T(8,128)(2,1)}, bf16[256,2048]{1,0:T(8,128)(2,1)}, bf16[64,512]{1,0:T(8,128)(2,1)}, bf16[64,512]{1,0:T(8,128)(2,1)}) custom-call(bf16[256,2048]{1,0:T(8,128)(2,1)S(1)} %get-tuple-element.28.refs_0_, bf16[256,2048]{1,0:T(8,128)(2,1)S(1)} %get-tuple-element.29.refs_1_, bf16[64,512]{1,0:T(8,128)(2,1)S(1)} %get-tuple-element.30.refs_2_, ...), custom_call_target="tpu_custom_call" | custom-call | tf_op jit(solution)/shard_map/output/pallas_call | solution.py:506
Async XLA Ops:
  0.6 0.8 copy-start.1
  1.5 0.8 copy-start.2
  43.9 0.8 copy-start
  44.7 0.7 copy-start.3

commit v4 on v3

--- a/solution.py
+++ b/solution.py
@@ -368,46 +368,72 @@
         copy.wait()
 
 
-def attend(count, unroll, z_blocks, head, start, q, g, k, v, wt, ds, dk, dv, picked):
+def attend(count, unroll, z_blocks, head, start, q, g, k, v, wt, ds, dk, dv, picked, held):
     lanes = columns(head, HEAD_WIDTH)
     nt = (((1,), (1,)), ((), ()))
-    results = []
+    items = []
     for u in range(unroll):
         qi = start + u
         block = qi // 4 * (z_blocks * 4) + qi % 4
-        chosen = [picked(head, j, block) for j in range(count)]
-        query = q[qi, :, lanes]
-        grad = g[qi, :, lanes]
-        scores = lax.dot_general(
-            jnp.concatenate([k[b] for b in chosen], 0), query, nt, preferred_element_type=jnp.float32
-        )
-        dweights = lax.dot_general(
-            jnp.concatenate([v[b] for b in chosen], 0), grad, nt, preferred_element_type=jnp.float32
-        )
-        peak = jnp.max(scores, axis=0, keepdims=True)
-        powers = jnp.exp2((scores - peak) * SCALE_LOG2E)
-        weights = powers * (1.0 / jnp.sum(powers, axis=0, keepdims=True))
-        delta = jnp.sum(weights * dweights, axis=0, keepdims=True)
-        dscores = (weights * (dweights - delta)).astype(jnp.bfloat16)
-        weights = weights.astype(jnp.bfloat16)
-        item = qi * 4 + head
-        wt[item, : count * BLOCK] = weights
-        ds[item, : count * BLOCK] = dscores
+        items.append((qi, [picked(head, j, block) for j in range(count)]))
+
+    def products(n):
+        qi, chosen = items[n]
+        for j, b in enumerate(chosen):
+            rows = slice(j * BLOCK, (j + 1) * BLOCK)
+            held[n % 2, 0, rows] = lax.dot_general(
+                k[b], q[qi, :, lanes], nt, preferred_element_type=jnp.float32
+            )
+            held[n % 2, 1, rows] = lax.dot_general(
+                v[b], g[qi, :, lanes], nt, preferred_element_type=jnp.float32
+            )
+
+    def softmax(n):
+        qi, chosen = items[n]
+        parts = [slice(j * BLOCK, (j + 1) * BLOCK) for j in range(count)]
+        peak = functools.reduce(jnp.maximum, [held[n % 2, 0, rows] for rows in parts])
+        peak = jnp.max(peak, axis=0, keepdims=True)
+        total = delta = 0.0
+        for rows in parts:
+            powers = jnp.exp2((held[n % 2, 0, rows] - peak) * SCALE_LOG2E)
+            held[n % 2, 0, rows] = powers
+            total = total + powers
+            delta = delta + powers * held[n % 2, 1, rows]
+        inverse = 1.0 / jnp.sum(total, axis=0, keepdims=True)
+        delta = jnp.sum(delta, axis=0, keepdims=True) * inverse
+        for rows in parts:
+            weights = held[n % 2, 0, rows] * inverse
+            wt[qi * 4 + head, rows] = weights.astype(jnp.bfloat16)
+            ds[qi * 4 + head, rows] = (weights * (held[n % 2, 1, rows] - delta)).astype(
+                jnp.bfloat16
+            )
         if count < 4:
             rest = jnp.zeros(((4 - count) * BLOCK, BLOCK), jnp.bfloat16)
-            wt[item, count * BLOCK :] = rest
-            ds[item, count * BLOCK :] = rest
-        dkey = jnp.dot(dscores, query, preferred_element_type=jnp.float32)
-        dvalue = jnp.dot(weights, grad, preferred_element_type=jnp.float32)
-        results.append((chosen, dkey, dvalue))
-    for chosen, dkey, dvalue in results:
+            wt[qi * 4 + head, count * BLOCK :] = rest
+            ds[qi * 4 + head, count * BLOCK :] = rest
+
+    def gradients(n):
+        qi, chosen = items[n]
         for j, b in enumerate(chosen):
             rows = slice(j * BLOCK, (j + 1) * BLOCK)
-            dk[b] += dkey[rows]
-            dv[b] += dvalue[rows]
-
-
-def attention_kernel(ring, unroll, lists, counts, q, g, k, v, wt, ds, dk, dv, own_lists, sem):
+            dk[b] += jnp.dot(
+                ds[qi * 4 + head, rows], q[qi, :, lanes], preferred_element_type=jnp.float32
+            )
+            dv[b] += jnp.dot(
+                wt[qi * 4 + head, rows], g[qi, :, lanes], preferred_element_type=jnp.float32
+            )
+
+    products(0)
+    for n in range(unroll):
+        if n + 1 < unroll:
+            products(n + 1)
+        if n > 0:
+            gradients(n - 1)
+        softmax(n)
+    gradients(unroll - 1)
+
+
+def attention_kernel(ring, unroll, lists, counts, q, g, k, v, wt, ds, dk, dv, held, own_lists, sem):
     place = Place(ring)
     copy = pltpu.make_async_copy(lists.at[pl.ds(place.head * 4, 4)], own_lists, sem)
     copy.start()
@@ -431,10 +457,26 @@
             def _():
                 @pl.loop(0, 8, step=unroll)
                 def _(start):
-                    attend(count, unroll, ring, head, start, q, g, k, v, wt, ds, dk, dv, picked)
-
-
-def attention(ring, lists, counts, qg, gg, kf, vf, unroll=2):
+                    attend(
+                        count,
+                        unroll,
+                        ring,
+                        head,
+                        start,
+                        q,
+                        g,
+                        k,
+                        v,
+                        wt,
+                        ds,
+                        dk,
+                        dv,
+                        picked,
+                        held,
+                    )
+
+
+def attention(ring, lists, counts, qg, gg, kf, vf, unroll=8):
     items = jax.ShapeDtypeStruct((32, 4 * BLOCK, BLOCK), jnp.bfloat16)
     rows = jax.ShapeDtypeStruct(kf.shape, jnp.float32)
     return pl.pallas_call(
@@ -443,6 +485,7 @@
         in_specs=[ANY_SPEC, pl.BlockSpec(memory_space=pltpu.SMEM)] + [VMEM_SPEC] * 4,
         out_specs=(VMEM_SPEC,) * 4,
         scratch_shapes=[
+            pltpu.VMEM((2, 2, 4 * BLOCK, BLOCK), jnp.float32),
             pltpu.SMEM((4, 4, lists.shape[2]), jnp.int32),
             pltpu.SemaphoreType.DMA,
         ],

time: 100 us -> 92.6 us (0.926)
  Pallas kernels: 96 us -> 88.9 us
    pallas_call x1, Pallas kernels: 39.9 us -> 36.3 us  [local(): pl.pallas_call(functools.partial(scatter_kernel, ring), out_shape=outs, i...]
    pallas_call x1, Pallas kernels: 13.1 us -> 9.62 us  [attention(): pl.pallas_call(functools.partial(attention_kernel, ring, unroll), out_sha...]
where the time goes in v4:
time: 92.6 us; the launch traced here: 92.7 us
  Pallas kernels  88.9 us (96%)
  local copies, waits for them, and re-layouts  3.08 us (3%)
    pallas_call x1, Pallas kernels, local(): pl.pallas_call(functools.partial(gather_kernel, ring), out_shape=(tokens,...  41.6 us
    pallas_call x1, Pallas kernels, local(): pl.pallas_call(functools.partial(scatter_kernel, ring), out_shape=outs, i...  36.3 us
    pallas_call x1, Pallas kernels, attention(): pl.pallas_call(functools.partial(attention_kernel, ring, unroll), out_sha...  9.62 us
    unnamed x8, local copies, waits for them, and re-layouts  3.08 us

profile of v4, /device:TPU:1, one launch (start us, length us, event | category | flops | bytes accessed | tf_op | source)
XLA Modules:
  0.0 92.7 jit_solution(18429682703342628285)
XLA Ops:
  0.6 0.0 copy-start.1
  0.6 0.8 copy-done.1
  1.5 0.0 copy-start.2
  1.5 0.8 copy-done.2
  2.3 41.6 %gather.1 = (bf16[4,256,512]{2,1,0:T(8,128)(2,1)S(1)}, bf16[4,256,512]{2,1,0:T(8,128)(2,1)S(1)}, bf16[32,128,128]{2,1,0:T(8,128)(2,1)S(1)}, bf16[32,128,128]{2,1...) custom-call(bf16[256,2048]{1,0:T(8,128)(2,1)} %q.1, bf16[256,2048]{1,0:T(8,128)(2,1)} %g.1, ...), custom_call_target="tpu_custom_call" | custom-call | tf_op jit(solution)/shard_map/gather/pallas_call | solution.py:515
  43.9 0.0 copy-start
  43.9 0.7 copy-done
  44.7 0.0 copy-start.3
  44.7 0.7 copy-done.3
  45.3 9.6 %attention.1 = (bf16[32,512,128]{2,1,0:T(8,128)(2,1)S(1)}, bf16[32,512,128]{2,1,0:T(8,128)(2,1)S(1)}, f32[32,128,128]{2,1,0:T(8,128)S(1)}, f32[32,128,128]{2,1,0:T(8,128)S(1)}) custom-call(s32[16,4,128]{2,1,0:T(4,128)S(1)} %bitcast.5, s32[16]{0:T(128)S(1)} %copy-done.3, bf16[8,128,512]{2,1,0:T(8,128)(2,1)S(1)} %bitcast.3, bf16[8,128,512]{2,1,0:T(8,128)(2,1)S(1)} %bitcast.4, ...), custom_call_target="tpu_custom_call" | custom-call | tf_op jit(solution)/shard_map/attention/pallas_call | solution.py:482
  55.0 36.3 %scatter.1 = (bf16[256,2048]{1,0:T(8,128)(2,1)S(1)}, bf16[256,2048]{1,0:T(8,128)(2,1)S(1)}, bf16[64,512]{1,0:T(8,128)(2,1)S(1)}, bf16[64,512]{1,0:T(8,128)(2,1)S(1)}) custom-call(s32[16,4,128]{2,1,0:T(4,128)S(1)} %bitcast.6, bf16[32,512,128]{2,1,0:T(8,128)(2,1)S(1)} %get-tuple-element.22.wt, bf16[32,512,128]{2,1,0:T(8,128)(2,1)S(1)} %get-tuple-element.23.ds, ...), custom_call_target="tpu_custom_call" | custom-call | tf_op jit(solution)/shard_map/scatter/pallas_call | solution.py:529
  91.3 1.4 %output.1 = (bf16[256,2048]{1,0:T(8,128)(2,1)}, bf16[256,2048]{1,0:T(8,128)(2,1)}, bf16[64,512]{1,0:T(8,128)(2,1)}, bf16[64,512]{1,0:T(8,128)(2,1)}) custom-call(bf16[256,2048]{1,0:T(8,128)(2,1)S(1)} %get-tuple-element.28.refs_0_, bf16[256,2048]{1,0:T(8,128)(2,1)S(1)} %get-tuple-element.29.refs_1_, bf16[64,512]{1,0:T(8,128)(2,1)S(1)} %get-tuple-element.30.refs_2_, ...), custom_call_target="tpu_custom_call" | custom-call | tf_op jit(solution)/shard_map/output/pallas_call | solution.py:549
Async XLA Ops:
  0.6 0.8 copy-start.1
  1.5 0.8 copy-start.2
  43.9 0.8 copy-start
  44.7 0.7 copy-start.3

commit v5 on v4

--- a/solution.py
+++ b/solution.py
@@ -67,6 +67,7 @@
 
 SIGNS = (1, -1)
 PIECES = [(t, i) for i in (2, 3, 1, 0) for t in range(2)]
+BLOCKS = [(t, flip) for flip in range(2) for t in range(2)]
 
 
 def gather_kernel(
@@ -130,14 +131,28 @@
             large.append(copy)
             copy.start()
 
-    def hop(way, chunk, slot, t, i):
-        piece = rows((kf, vf)[t], ROUTES[i], chunk_z(way, chunk))
+    def block_of(flip, z):
+        member = 1 - place.member if flip else place.member
+        return member * ring + z
+
+    def hop(way, chunk, slot, t, flip):
+        block = (kf, vf)[t].at[block_of(flip, chunk_z(way, chunk))]
+        return remote(
+            block,
+            block,
+            send_z.at[way, slot, t * 2 + flip],
+            recv_z.at[way, slot, t * 2 + flip],
+            place.partner(ROUTES[0], SIGNS[way])[3],
+        )
+
+    def first_arrival(way, t, i):
+        piece = rows((kf, vf)[t], ROUTES[i], chunk_z(way, 1))
         return remote(
             piece,
             piece,
-            send_z.at[way, slot, t * 4 + i],
-            recv_z.at[way, slot, t * 4 + i],
-            place.partner(ROUTES[0], SIGNS[way])[3],
+            send_z.at[way, 0, t * 4 + i],
+            recv_z.at[way, 0, t * 4 + i],
+            place.partner(ROUTES[i], SIGNS[way])[3],
         )
 
     def turn(z):
@@ -146,41 +161,49 @@
             kt[block] = kf[block].T
             vt[block] = vf[block].T
 
+    for t, flip in BLOCKS:
+        for way in range(2):
+            for core in range(2):
+                first_arrival(way, t, 2 * flip + core).wait_recv()
+            hop(way, 1, 1, t, flip).start()
+    for way in range(2):
+        turn(chunk_z(way, 1))
+
     def forward(step, carry):
-        for t, i in reversed(PIECES):
+        for t, flip in BLOCKS:
             for way in range(2):
-                hop(way, step, step - 1, t, i).wait_recv()
-                hop(way, step, step, t, i).start()
+                hop(way, step, step - 1, t, flip).wait_recv()
+                hop(way, step, step, t, flip).start()
         for way in range(2):
             turn(chunk_z(way, step))
         return carry
 
-    lax.fori_loop(1, far - 1, forward, 0)
-    for t, i in reversed(PIECES):
-        for way in range(2):
-            hop(way, far - 1, far - 2, t, i).wait_recv()
-            if i % 2 == way:
-                hop(way, far - 1, far - 1, t, i).start()
+    lax.fori_loop(2, far - 1, forward, 0)
+    for t, flip in BLOCKS:
+        for way in range(2):
+            hop(way, far - 1, far - 2, t, flip).wait_recv()
+            if flip == way:
+                hop(way, far - 1, far - 1, t, flip).start()
     for way in range(2):
         turn(chunk_z(way, far - 1))
     for i, copy in near:
         copy.wait() if i == 0 else copy.wait_recv()
     turn(place.z)
-    for t, i in reversed(PIECES):
-        hop(i % 2, far, far - 1, t, i).wait_recv()
+    for t, flip in BLOCKS:
+        hop(flip, far, far - 1, t, flip).wait_recv()
     turn(chunk_z(0, far))
 
     def drain(step, carry):
-        for t, i in PIECES:
+        for t, flip in BLOCKS:
             for way in range(2):
-                hop(way, step, step, t, i).wait_send()
+                hop(way, step, step, t, flip).wait_send()
         return carry
 
     for copy in first:
         copy.wait_send()
     lax.fori_loop(1, far - 1, drain, 0)
-    for t, i in PIECES:
-        hop(i % 2, far - 1, far - 1, t, i).wait_send()
+    for t, flip in BLOCKS:
+        hop(flip, far - 1, far - 1, t, flip).wait_send()
     for i, copy in near:
         if i > 0:
             copy.wait_send()
@@ -206,6 +229,7 @@
     first,
     own,
     landed,
+    arrived,
     own_lists,
     list_sem,
     own_sem,
@@ -221,45 +245,60 @@
     half = dko.shape[0]
     far = ring // 2
 
-    def partial(way, distance, t, i):
-        member, core, _, _ = place.partner(ROUTES[i])
+    def partial(way, distance, t, flip):
+        member = 1 - place.member if flip else place.member
         z = (place.z + SIGNS[way] * distance + ring) % ring
-        return (dk, dv)[t][member * ring + z, columns(core, half), :]
-
-    def longer(way, i):
-        return i % 2 == way
-
-    for t, i in PIECES:
-        for way in range(2):
-            distance = far if longer(way, i) else far - 1
-            first[way, t * 4 + i] = partial(way, distance, t, i).astype(jnp.bfloat16)
+        return (dk, dv)[t].at[member * ring + z]
+
+    def start_distance(way, flip):
+        return far if flip == way else far - 1
+
+    for t, flip in BLOCKS:
+        for way in range(2):
+            block = partial(way, start_distance(way, flip), t, flip)
+            first[way, t * 2 + flip] = block[...].astype(jnp.bfloat16)
     pl.semaphore_wait(barrier, expected)
 
-    def hop(source, way, slot, t, i, last=False):
+    def hop(source, way, slot, t, flip):
         return remote(
             source,
-            landed.at[way, slot, t * 4 + i],
-            send_z.at[way, slot, t * 4 + i],
-            recv_z.at[way, slot, t * 4 + i],
-            place.partner(ROUTES[i if last else 0], SIGNS[way])[3],
+            landed.at[way, slot, t * 2 + flip],
+            send_z.at[way, slot, t * 2 + flip],
+            recv_z.at[way, slot, t * 2 + flip],
+            place.partner(ROUTES[0], SIGNS[way])[3],
         )
 
-    def pass_on(way, distance, t, i, last=False):
-        slot = landed.at[way, distance, t * 4 + i]
-        hop(slot, way, distance, t, i).wait_recv()
-        slot[...] = (slot[...].astype(jnp.float32) + partial(way, distance, t, i)).astype(
+    def last_hop(way, t, i):
+        core = place.partner(ROUTES[i])[1]
+        return remote(
+            landed.at[way, 1, t * 2 + i // 2, columns(core, half), :],
+            arrived.at[way, t * 4 + i],
+            send_z.at[way, 0, t * 4 + i],
+            recv_z.at[way, 0, t * 4 + i],
+            place.partner(ROUTES[i], SIGNS[way])[3],
+        )
+
+    def pass_on(way, distance, t, flip, last=False):
+        slot = landed.at[way, distance, t * 2 + flip]
+        hop(slot, way, distance, t, flip).wait_recv()
+        slot[...] = (slot[...].astype(jnp.float32) + partial(way, distance, t, flip)[...]).astype(
             jnp.bfloat16
         )
-        hop(slot, way, distance - 1, t, i, last).start()
-
-    for t, i in PIECES:
-        for way in range(2):
-            distance = far if longer(way, i) else far - 1
-            hop(first.at[way, t * 4 + i], way, distance - 1, t, i).start()
+        if last:
+            for core in range(2):
+                last_hop(way, t, 2 * flip + core).start()
+        else:
+            hop(slot, way, distance - 1, t, flip).start()
+
+    for t, flip in BLOCKS:
+        for way in range(2):
+            slot = start_distance(way, flip) - 1
+            hop(first.at[way, t * 2 + flip], way, slot, t, flip).start()
     copies = []
     for t, i in PIECES:
         piece = t * 4 + i
-        own[0, piece] = partial(0, 0, t, i).astype(jnp.bfloat16)
+        core = place.partner(ROUTES[i])[1]
+        own[0, piece] = partial(0, 0, t, i // 2)[columns(core, half), :].astype(jnp.bfloat16)
         if i > 0:
             copies.append(
                 remote(
@@ -305,32 +344,32 @@
 
     list_copy.wait()
     finish(2)
-    for t, i in PIECES:
-        pass_on(i % 2, far - 1, t, i)
+    for t, flip in BLOCKS:
+        pass_on(flip, far - 1, t, flip)
     finish(3)
     for distance in (far - 2, far - 3):
-        for t, i in PIECES:
+        for t, flip in BLOCKS:
             for way in range(2):
-                pass_on(way, distance, t, i)
+                pass_on(way, distance, t, flip)
         finish(far - 1 - distance if distance == far - 2 else 0)
 
     def steps(n, carry):
-        for t, i in PIECES:
+        for t, flip in BLOCKS:
             for way in range(2):
-                pass_on(way, far - 4 - n, t, i)
+                pass_on(way, far - 4 - n, t, flip)
         return carry
 
     lax.fori_loop(0, far - 5, steps, 0)
-    for t, i in PIECES:
-        for way in range(2):
-            pass_on(way, 1, t, i, True)
+    for t, flip in reversed(BLOCKS):
+        for way in range(2):
+            pass_on(way, 1, t, flip, True)
     for copy in copies[:6]:
         copy.wait_recv()
     for t, i in reversed(PIECES):
         piece = t * 4 + i
         for way in range(2):
-            hop(landed.at[way, 0, piece], way, 0, t, i, True).wait_recv()
-        total = landed[0, 0, piece].astype(jnp.float32) + landed[1, 0, piece].astype(jnp.float32)
+            last_hop(way, t, i).wait_recv()
+        total = arrived[0, piece].astype(jnp.float32) + arrived[1, piece].astype(jnp.float32)
         total = total + own[1 if i > 0 else 0, piece].astype(jnp.float32)
         if t == 0:
             total = total * SCALE
@@ -339,16 +378,17 @@
         )
 
     def drain(step, carry):
-        for t, i in PIECES:
+        for t, flip in BLOCKS:
             for way in range(2):
-                hop(landed.at[way, step, t * 4 + i], way, step, t, i).wait_send()
+                hop(landed.at[way, step, t * 2 + flip], way, step, t, flip).wait_send()
         return carry
 
     lax.fori_loop(1, far - 1, drain, 0)
+    for t, flip in BLOCKS:
+        hop(landed.at[flip, far - 1, t * 2 + flip], flip, far - 1, t, flip).wait_send()
     for t, i in PIECES:
         for way in range(2):
-            hop(landed.at[way, 0, t * 4 + i], way, 0, t, i, True).wait_send()
-        hop(landed.at[i % 2, far - 1, t * 4 + i], i % 2, far - 1, t, i).wait_send()
+            last_hop(way, t, i).wait_send()
     for n, copy in enumerate(copies):
         if n < 6:
             copy.wait_send()
@@ -522,7 +562,7 @@
             collective_id=0, has_side_effects=True, vmem_limit_bytes=47 << 20
         ),
         name="gather",
-    )(queries, grad_out, keys, values)
+    )(queries, grad_out, *(pltpu.with_memory_space_constraint(x, pltpu.HBM) for x in (keys, values)))
     shape = (8, BLOCK, GROUP_WIDTH)
     lists = layout.transpose(0, 2, 1)
     wt, ds, dk, dv = attention(ring, lists, counts, qg.reshape(shape), gg.reshape(shape), kf, vf)
@@ -534,9 +574,10 @@
         scratch_shapes=[
             pltpu.VMEM(tokens.shape, jnp.bfloat16),
             pltpu.VMEM(tokens.shape, jnp.bfloat16),
+            pltpu.VMEM((2, 4, BLOCK, HEAD_WIDTH), jnp.bfloat16),
             pltpu.VMEM((2, 8, half, HEAD_WIDTH), jnp.bfloat16),
+            pltpu.VMEM((2, ring // 2, 4, BLOCK, HEAD_WIDTH), jnp.bfloat16),
             pltpu.VMEM((2, 8, half, HEAD_WIDTH), jnp.bfloat16),
-            pltpu.VMEM((2, ring // 2, 8, half, HEAD_WIDTH), jnp.bfloat16),
             pltpu.SMEM((4, 4, lists.shape[2]), jnp.int32),
             pltpu.SemaphoreType.DMA,
         ]

time: 92.6 us -> 95.1 us (1.027); the launches traced: 92.7 us -> 94 us
  Pallas kernels: 88.9 us -> 91.9 us
  local copies, waits for them, and re-layouts: 3.08 us -> 1.41 us
    pallas_call x1, Pallas kernels: 36.3 us -> 39.3 us  [local(): pl.pallas_call(functools.partial(scatter_kernel, ring), out_shape=outs, i...]
    unnamed x8 -> x4, local copies, waits for them, and re-layouts: 3.08 us -> 1.41 us
where the time goes in v5:
time: 95.1 us; the launch traced here: 94 us
  Pallas kernels  91.9 us (97%)
  local copies, waits for them, and re-layouts  1.41 us (1%)
    pallas_call x1, Pallas kernels, local(): pl.pallas_call(functools.partial(gather_kernel, ring), out_shape=(tokens,...  41.9 us
    pallas_call x1, Pallas kernels, local(): pl.pallas_call(functools.partial(scatter_kernel, ring), out_shape=outs, i...  39.3 us
    pallas_call x1, Pallas kernels, attention(): pl.pallas_call(functools.partial(attention_kernel, ring, unroll), out_sha...  9.36 us

profile of v5, /device:TPU:1, one launch (start us, length us, event | category | flops | bytes accessed | tf_op | source)
XLA Modules:
  0.0 94.0 jit_solution(6204234963049312685)
XLA Ops:
  0.6 41.9 %gather.1 = (bf16[4,256,512]{2,1,0:T(8,128)(2,1)S(1)}, bf16[4,256,512]{2,1,0:T(8,128)(2,1)S(1)}, bf16[32,128,128]{2,1,0:T(8,128)(2,1)S(1)}, bf16[32,128,128]{2,1...) custom-call(bf16[256,2048]{1,0:T(8,128)(2,1)} %q.1, bf16[256,2048]{1,0:T(8,128)(2,1)} %g.1, ...), custom_call_target="tpu_custom_call" | custom-call | tf_op jit(solution)/shard_map/gather/pallas_call | solution.py:555
  42.5 0.0 copy-start
  42.5 0.7 copy-done
  43.3 0.0 copy-start.1
  43.3 0.7 copy-done.1
  43.9 9.4 %attention.1 = (bf16[32,512,128]{2,1,0:T(8,128)(2,1)S(1)}, bf16[32,512,128]{2,1,0:T(8,128)(2,1)S(1)}, f32[32,128,128]{2,1,0:T(8,128)S(1)}, f32[32,128,128]{2,1,0:T(8,128)S(1)}) custom-call(s32[16,4,128]{2,1,0:T(4,128)S(1)} %bitcast.5, s32[16]{0:T(128)S(1)} %copy-done.1, bf16[8,128,512]{2,1,0:T(8,128)(2,1)S(1)} %bitcast.3, bf16[8,128,512]{2,1,0:T(8,128)(2,1)S(1)} %bitcast.4, ...), custom_call_target="tpu_custom_call" | custom-call | tf_op jit(solution)/shard_map/attention/pallas_call | solution.py:522
  53.3 39.3 %scatter.1 = (bf16[256,2048]{1,0:T(8,128)(2,1)S(1)}, bf16[256,2048]{1,0:T(8,128)(2,1)S(1)}, bf16[64,512]{1,0:T(8,128)(2,1)S(1)}, bf16[64,512]{1,0:T(8,128)(2,1)S(1)}) custom-call(s32[16,4,128]{2,1,0:T(4,128)S(1)} %bitcast.6, bf16[32,512,128]{2,1,0:T(8,128)(2,1)S(1)} %get-tuple-element.22.wt, bf16[32,512,128]{2,1,0:T(8,128)(2,1)S(1)} %get-tuple-element.23.ds, ...), custom_call_target="tpu_custom_call" | custom-call | tf_op jit(solution)/shard_map/scatter/pallas_call | solution.py:569
  92.6 1.4 %output.1 = (bf16[256,2048]{1,0:T(8,128)(2,1)}, bf16[256,2048]{1,0:T(8,128)(2,1)}, bf16[64,512]{1,0:T(8,128)(2,1)}, bf16[64,512]{1,0:T(8,128)(2,1)}) custom-call(bf16[256,2048]{1,0:T(8,128)(2,1)S(1)} %get-tuple-element.28.refs_0_, bf16[256,2048]{1,0:T(8,128)(2,1)S(1)} %get-tuple-element.29.refs_1_, bf16[64,512]{1,0:T(8,128)(2,1)S(1)} %get-tuple-element.30.refs_2_, ...), custom_call_target="tpu_custom_call" | custom-call | tf_op jit(solution)/shard_map/output/pallas_call | solution.py:590
Async XLA Ops:
  42.5 0.8 copy-start
  43.3 0.7 copy-start.1

commit v6 on v4

--- a/solution.py
+++ b/solution.py
@@ -67,6 +67,7 @@
 
 SIGNS = (1, -1)
 PIECES = [(t, i) for i in (2, 3, 1, 0) for t in range(2)]
+BLOCKS = [(t, flip) for flip in range(2) for t in range(2)]
 
 
 def gather_kernel(
@@ -130,14 +131,28 @@
             large.append(copy)
             copy.start()
 
-    def hop(way, chunk, slot, t, i):
-        piece = rows((kf, vf)[t], ROUTES[i], chunk_z(way, chunk))
+    def block_of(flip, z):
+        member = 1 - place.member if flip else place.member
+        return member * ring + z
+
+    def hop(way, chunk, slot, t, flip):
+        block = (kf, vf)[t].at[block_of(flip, chunk_z(way, chunk))]
+        return remote(
+            block,
+            block,
+            send_z.at[way, slot, t * 2 + flip],
+            recv_z.at[way, slot, t * 2 + flip],
+            place.partner(ROUTES[0], SIGNS[way])[3],
+        )
+
+    def first_arrival(way, t, i):
+        piece = rows((kf, vf)[t], ROUTES[i], chunk_z(way, 1))
         return remote(
             piece,
             piece,
-            send_z.at[way, slot, t * 4 + i],
-            recv_z.at[way, slot, t * 4 + i],
-            place.partner(ROUTES[0], SIGNS[way])[3],
+            send_z.at[way, 0, t * 4 + i],
+            recv_z.at[way, 0, t * 4 + i],
+            place.partner(ROUTES[i], SIGNS[way])[3],
         )
 
     def turn(z):
@@ -146,41 +161,49 @@
             kt[block] = kf[block].T
             vt[block] = vf[block].T
 
+    for t, flip in BLOCKS:
+        for way in range(2):
+            for core in range(2):
+                first_arrival(way, t, 2 * flip + core).wait_recv()
+            hop(way, 1, 1, t, flip).start()
+    for way in range(2):
+        turn(chunk_z(way, 1))
+
     def forward(step, carry):
-        for t, i in reversed(PIECES):
+        for t, flip in BLOCKS:
             for way in range(2):
-                hop(way, step, step - 1, t, i).wait_recv()
-                hop(way, step, step, t, i).start()
+                hop(way, step, step - 1, t, flip).wait_recv()
+                hop(way, step, step, t, flip).start()
         for way in range(2):
             turn(chunk_z(way, step))
         return carry
 
-    lax.fori_loop(1, far - 1, forward, 0)
-    for t, i in reversed(PIECES):
-        for way in range(2):
-            hop(way, far - 1, far - 2, t, i).wait_recv()
-            if i % 2 == way:
-                hop(way, far - 1, far - 1, t, i).start()
+    lax.fori_loop(2, far - 1, forward, 0)
+    for t, flip in BLOCKS:
+        for way in range(2):
+            hop(way, far - 1, far - 2, t, flip).wait_recv()
+            if flip == way:
+                hop(way, far - 1, far - 1, t, flip).start()
     for way in range(2):
         turn(chunk_z(way, far - 1))
     for i, copy in near:
         copy.wait() if i == 0 else copy.wait_recv()
     turn(place.z)
-    for t, i in reversed(PIECES):
-        hop(i % 2, far, far - 1, t, i).wait_recv()
+    for t, flip in BLOCKS:
+        hop(flip, far, far - 1, t, flip).wait_recv()
     turn(chunk_z(0, far))
 
     def drain(step, carry):
-        for t, i in PIECES:
+        for t, flip in BLOCKS:
             for way in range(2):
-                hop(way, step, step, t, i).wait_send()
+                hop(way, step, step, t, flip).wait_send()
         return carry
 
     for copy in first:
         copy.wait_send()
     lax.fori_loop(1, far - 1, drain, 0)
-    for t, i in PIECES:
-        hop(i % 2, far - 1, far - 1, t, i).wait_send()
+    for t, flip in BLOCKS:
+        hop(flip, far - 1, far - 1, t, flip).wait_send()
     for i, copy in near:
         if i > 0:
             copy.wait_send()
@@ -379,13 +402,12 @@
 
     def products(n):
         qi, chosen = items[n]
-        for j, b in enumerate(chosen):
-            rows = slice(j * BLOCK, (j + 1) * BLOCK)
-            held[n % 2, 0, rows] = lax.dot_general(
-                k[b], q[qi, :, lanes], nt, preferred_element_type=jnp.float32
-            )
-            held[n % 2, 1, rows] = lax.dot_general(
-                v[b], g[qi, :, lanes], nt, preferred_element_type=jnp.float32
+        for t, (source, other) in enumerate(((k, q), (v, g))):
+            held[n % 2, t, : count * BLOCK] = lax.dot_general(
+                jnp.concatenate([source[b] for b in chosen], 0),
+                other[qi, :, lanes],
+                nt,
+                preferred_element_type=jnp.float32,
             )
 
     def softmax(n):
@@ -414,14 +436,14 @@
 
     def gradients(n):
         qi, chosen = items[n]
-        for j, b in enumerate(chosen):
-            rows = slice(j * BLOCK, (j + 1) * BLOCK)
-            dk[b] += jnp.dot(
-                ds[qi * 4 + head, rows], q[qi, :, lanes], preferred_element_type=jnp.float32
+        for source, other, target in ((ds, q, dk), (wt, g, dv)):
+            product = jnp.dot(
+                source[qi * 4 + head, : count * BLOCK],
+                other[qi, :, lanes],
+                preferred_element_type=jnp.float32,
             )
-            dv[b] += jnp.dot(
-                wt[qi * 4 + head, rows], g[qi, :, lanes], preferred_element_type=jnp.float32
-            )
+            for j, b in enumerate(chosen):
+                target[b] += product[j * BLOCK : (j + 1) * BLOCK]
 
     products(0)
     for n in range(unroll):
@@ -433,24 +455,29 @@
     gradients(unroll - 1)
 
 
-def attention_kernel(ring, unroll, lists, counts, q, g, k, v, wt, ds, dk, dv, held, own_lists, sem):
+def attention_kernel(ring, unroll, lists, counts, q, g, k, v, wt, ds, dk, dv, held, own_lists, used_counts, sems):
     place = Place(ring)
-    copy = pltpu.make_async_copy(lists.at[pl.ds(place.head * 4, 4)], own_lists, sem)
-    copy.start()
+    copies = [
+        pltpu.make_async_copy(lists.at[pl.ds(place.head * 4, 4)], own_lists, sems.at[0]),
+        pltpu.make_async_copy(counts, used_counts, sems.at[1]),
+    ]
+    for copy in copies:
+        copy.start()
 
     @pl.loop(0, k.shape[0])
     def _(b):
         dk[b] = jnp.zeros((BLOCK, HEAD_WIDTH), jnp.float32)
         dv[b] = jnp.zeros((BLOCK, HEAD_WIDTH), jnp.float32)
 
-    copy.wait()
+    for copy in copies:
+        copy.wait()
 
     def picked(head, j, block):
         return own_lists[head, j, place.z * 4 + block]
 
     @pl.loop(0, 4)
     def _(head):
-        used = counts[place.head * 4 + head]
+        used = used_counts[place.head * 4 + head]
         for count in range(1, 5):
 
             @pl.when(used == count)
@@ -482,12 +509,13 @@
     return pl.pallas_call(
         functools.partial(attention_kernel, ring, unroll),
         out_shape=(items, items, rows, rows),
-        in_specs=[ANY_SPEC, pl.BlockSpec(memory_space=pltpu.SMEM)] + [VMEM_SPEC] * 4,
+        in_specs=[HBM_SPEC, HBM_SPEC] + [VMEM_SPEC] * 4,
         out_specs=(VMEM_SPEC,) * 4,
         scratch_shapes=[
             pltpu.VMEM((2, 2, 4 * BLOCK, BLOCK), jnp.float32),
             pltpu.SMEM((4, 4, lists.shape[2]), jnp.int32),
-            pltpu.SemaphoreType.DMA,
+            pltpu.SMEM(counts.shape, jnp.int32),
+            pltpu.SemaphoreType.DMA((2,)),
         ],
         compiler_params=pltpu.CompilerParams(vmem_limit_bytes=32 << 20),
         name="attention",
@@ -502,6 +530,10 @@
         pltpu.SemaphoreType.DMA((2, ring // 2, 8)),
         pltpu.SemaphoreType.DMA((2, ring // 2, 8)),
     ]
+
+
+def in_hbm(x):
+    return pltpu.with_memory_space_constraint(x, pltpu.HBM)
 
 
 def local(queries, keys, values, grad_out, layout, counts):
@@ -522,14 +554,15 @@
             collective_id=0, has_side_effects=True, vmem_limit_bytes=47 << 20
         ),
         name="gather",
-    )(queries, grad_out, keys, values)
+    )(queries, grad_out, in_hbm(keys), in_hbm(values))
     shape = (8, BLOCK, GROUP_WIDTH)
-    lists = layout.transpose(0, 2, 1)
+    lists = in_hbm(layout.transpose(0, 2, 1))
+    counts = in_hbm(counts)
     wt, ds, dk, dv = attention(ring, lists, counts, qg.reshape(shape), gg.reshape(shape), kf, vf)
     results = pl.pallas_call(
         functools.partial(scatter_kernel, ring),
         out_shape=outs,
-        in_specs=[ANY_SPEC] + [VMEM_SPEC] * 6,
+        in_specs=[HBM_SPEC] + [VMEM_SPEC] * 6,
         out_specs=(VMEM_SPEC,) * 4,
         scratch_shapes=[
             pltpu.VMEM(tokens.shape, jnp.bfloat16),

time: 92.6 us -> 89.2 us (0.963)
  local copies, waits for them, and re-layouts: 3.08 us -> 0 us
    unnamed x8 -> x0, local copies, waits for them, and re-layouts: 3.08 us -> none
    pallas_call x1, Pallas kernels: 9.62 us -> 6.81 us  [attention(): pl.pallas_call(functools.partial(attention_kernel, ring, unroll), out_sha...]
    pallas_call x1, Pallas kernels: 36.3 us -> 37.9 us  [local(): pl.pallas_call(functools.partial(scatter_kernel, ring), out_shape=outs, i...]
where the time goes in v6:
time: 89.2 us; the launch traced here: 88.6 us
  Pallas kernels  88 us (99%)
    pallas_call x1, Pallas kernels, local(): pl.pallas_call(functools.partial(gather_kernel, ring), out_shape=(tokens,...  41.9 us
    pallas_call x1, Pallas kernels, local(): pl.pallas_call(functools.partial(scatter_kernel, ring), out_shape=outs, i...  37.9 us
    pallas_call x1, Pallas kernels, attention(): pl.pallas_call(functools.partial(attention_kernel, ring, unroll), out_sha...  6.81 us

profile of v6, /device:TPU:1, one launch (start us, length us, event | category | flops | bytes accessed | tf_op | source)
XLA Modules:
  0.0 88.6 jit_solution(12895486436581212413)
XLA Ops:
  0.6 41.9 %gather.1 = (bf16[4,256,512]{2,1,0:T(8,128)(2,1)S(1)}, bf16[4,256,512]{2,1,0:T(8,128)(2,1)S(1)}, bf16[32,128,128]{2,1,0:T(8,128)(2,1)S(1)}, bf16[32,128,128]{2,1...) custom-call(bf16[256,2048]{1,0:T(8,128)(2,1)} %q.1, bf16[256,2048]{1,0:T(8,128)(2,1)} %g.1, ...), custom_call_target="tpu_custom_call" | custom-call | tf_op jit(solution)/shard_map/gather/pallas_call | solution.py:547
  42.5 6.8 %attention.1 = (bf16[32,512,128]{2,1,0:T(8,128)(2,1)S(1)}, bf16[32,512,128]{2,1,0:T(8,128)(2,1)S(1)}, f32[32,128,128]{2,1,0:T(8,128)S(1)}, f32[32,128,128]{2,1,0:T(8,128)S(1)}) custom-call(s32[16,4,128]{2,1,0:T(4,128)} %bitcast.5, s32[16]{0:T(128)} %counts.1, bf16[8,128,512]{2,1,0:T(8,128)(2,1)S(1)} %bitcast.3, bf16[8,128,512]{2,1,0:T(8,128)(2,1)S(1)} %bitcast.4, ...), custom_call_target="tpu_custom_call" | custom-call | tf_op jit(solution)/shard_map/attention/pallas_call | solution.py:509
  49.3 37.9 %scatter.1 = (bf16[256,2048]{1,0:T(8,128)(2,1)S(1)}, bf16[256,2048]{1,0:T(8,128)(2,1)S(1)}, bf16[64,512]{1,0:T(8,128)(2,1)S(1)}, bf16[64,512]{1,0:T(8,128)(2,1)S(1)}) custom-call(s32[16,4,128]{2,1,0:T(4,128)} %bitcast.6, bf16[32,512,128]{2,1,0:T(8,128)(2,1)S(1)} %get-tuple-element.22.wt, bf16[32,512,128]{2,1,0:T(8,128)(2,1)S(1)} %get-tuple-element.23.ds, ...), custom_call_target="tpu_custom_call" | custom-call | tf_op jit(solution)/shard_map/scatter/pallas_call | solution.py:562
  87.3 1.4 %output.1 = (bf16[256,2048]{1,0:T(8,128)(2,1)}, bf16[256,2048]{1,0:T(8,128)(2,1)}, bf16[64,512]{1,0:T(8,128)(2,1)}, bf16[64,512]{1,0:T(8,128)(2,1)}) custom-call(bf16[256,2048]{1,0:T(8,128)(2,1)S(1)} %get-tuple-element.28.refs_0_, bf16[256,2048]{1,0:T(8,128)(2,1)S(1)} %get-tuple-element.29.refs_1_, bf16[64,512]{1,0:T(8,128)(2,1)S(1)} %get-tuple-element.30.refs_2_, ...), custom_call_target="tpu_custom_call" | custom-call | tf_op jit(solution)/shard_map/output/pallas_call | solution.py:582

commit v7 on v6

--- a/solution.py
+++ b/solution.py
@@ -178,7 +178,8 @@
             turn(chunk_z(way, step))
         return carry
 
-    lax.fori_loop(2, far - 1, forward, 0)
+    for step in range(2, far - 1):
+        forward(step, 0)
     for t, flip in BLOCKS:
         for way in range(2):
             hop(way, far - 1, far - 2, t, flip).wait_recv()
@@ -343,7 +344,8 @@
                 pass_on(way, far - 4 - n, t, i)
         return carry
 
-    lax.fori_loop(0, far - 5, steps, 0)
+    for n in range(far - 5):
+        steps(n, 0)
     for t, i in PIECES:
         for way in range(2):
             pass_on(way, 1, t, i, True)

time: 89.2 us -> 89 us (level)
    pallas_call x1, Pallas kernels: 37.9 us -> 36.5 us  [local(): pl.pallas_call(functools.partial(scatter_kernel, ring), out_shape=outs, i...]
    pallas_call x1, Pallas kernels: 6.81 us -> 7.8 us  [attention(): pl.pallas_call(functools.partial(attention_kernel, ring, unroll), out_sha...]
where the time goes in v7:
time: 89 us; the launch traced here: 88.2 us
  Pallas kernels  87.5 us (98%)
    pallas_call x1, Pallas kernels, local(): pl.pallas_call(functools.partial(gather_kernel, ring), out_shape=(tokens,...  41.9 us
    pallas_call x1, Pallas kernels, local(): pl.pallas_call(functools.partial(scatter_kernel, ring), out_shape=outs, i...  36.5 us
    pallas_call x1, Pallas kernels, attention(): pl.pallas_call(functools.partial(attention_kernel, ring, unroll), out_sha...  7.8 us

profile of v7, /device:TPU:1, one launch (start us, length us, event | category | flops | bytes accessed | tf_op | source)
XLA Modules:
  0.0 88.2 jit_solution(16689576403051822096)
XLA Ops:
  0.6 41.9 %gather.1 = (bf16[4,256,512]{2,1,0:T(8,128)(2,1)S(1)}, bf16[4,256,512]{2,1,0:T(8,128)(2,1)S(1)}, bf16[32,128,128]{2,1,0:T(8,128)(2,1)S(1)}, bf16[32,128,128]{2,1...) custom-call(bf16[256,2048]{1,0:T(8,128)(2,1)} %q.1, bf16[256,2048]{1,0:T(8,128)(2,1)} %g.1, ...), custom_call_target="tpu_custom_call" | custom-call | tf_op jit(solution)/shard_map/gather/pallas_call | solution.py:549
  42.5 7.8 %attention.1 = (bf16[32,512,128]{2,1,0:T(8,128)(2,1)S(1)}, bf16[32,512,128]{2,1,0:T(8,128)(2,1)S(1)}, f32[32,128,128]{2,1,0:T(8,128)S(1)}, f32[32,128,128]{2,1,0:T(8,128)S(1)}) custom-call(s32[16,4,128]{2,1,0:T(4,128)} %bitcast.5, s32[16]{0:T(128)} %counts.1, bf16[8,128,512]{2,1,0:T(8,128)(2,1)S(1)} %bitcast.3, bf16[8,128,512]{2,1,0:T(8,128)(2,1)S(1)} %bitcast.4, ...), custom_call_target="tpu_custom_call" | custom-call | tf_op jit(solution)/shard_map/attention/pallas_call | solution.py:511
  50.3 36.5 %scatter.1 = (bf16[256,2048]{1,0:T(8,128)(2,1)S(1)}, bf16[256,2048]{1,0:T(8,128)(2,1)S(1)}, bf16[64,512]{1,0:T(8,128)(2,1)S(1)}, bf16[64,512]{1,0:T(8,128)(2,1)S(1)}) custom-call(s32[16,4,128]{2,1,0:T(4,128)} %bitcast.6, bf16[32,512,128]{2,1,0:T(8,128)(2,1)S(1)} %get-tuple-element.22.wt, bf16[32,512,128]{2,1,0:T(8,128)(2,1)S(1)} %get-tuple-element.23.ds, ...), custom_call_target="tpu_custom_call" | custom-call | tf_op jit(solution)/shard_map/scatter/pallas_call | solution.py:564
  86.8 1.4 %output.1 = (bf16[256,2048]{1,0:T(8,128)(2,1)}, bf16[256,2048]{1,0:T(8,128)(2,1)}, bf16[64,512]{1,0:T(8,128)(2,1)}, bf16[64,512]{1,0:T(8,128)(2,1)}) custom-call(bf16[256,2048]{1,0:T(8,128)(2,1)S(1)} %get-tuple-element.28.refs_0_, bf16[256,2048]{1,0:T(8,128)(2,1)S(1)} %get-tuple-element.29.refs_1_, bf16[64,512]{1,0:T(8,128)(2,1)S(1)} %get-tuple-element.30.refs_2_, ...), custom_call_target="tpu_custom_call" | custom-call | tf_op jit(solution)/shard_map/output/pallas_call | solution.py:584
